TPU v7x, 128 devices: a whole 4x4x4 slice. The times are simulated.
128 devices in a mesh: gx: 16 (over z, x), gy: 8 (over y, core).
Axes of the slice: x: 4, y: 4, z: 4, core: 2. Of those that a mesh axis runs over, the one named last changes fastest.
Arguments:
- cotangent: float32 [16, 8, 42, 1024], P('gx', 'gy'), may hold values from -6 to 6
- section_states: bfloat16 [3, 16, 8, 42, 1024], P(None, 'gx', 'gy'), may hold values from -6 to 6
- inverse_area: float32 [16, 8, 1024], P('gx', 'gy'), may hold values from 0.5 to 2
- edge_length: float32 [16, 8, 3, 1024], P('gx', 'gy'), may hold values from 0.5 to 1.5
- roughness: float32 [16, 8, 1024], P('gx', 'gy'), may hold values from 0.5 to 2
- soil_conductance: float32 [16, 8, 1024], P('gx', 'gy'), may hold values from 0.5 to 2
- zone_friction: float32 [512], replicated, may hold values from 0.25 to 1
- zone_conductivity: float32 [512], replicated, may hold values from 0.25 to 1
- wet_mask: int32 [16, 8, 1024], P('gx', 'gy'), may hold values 0 or 1
- element_zone: int32 [16, 8, 1024], P('gx', 'gy'), may hold values from 0 to 511, as said below
- send_face: int32 [16, 8, 8, 256], P('gx', 'gy'), may hold values from 0 to 3071, as said below
- send_count: int32 [16, 8, 8], P('gx', 'gy'), may hold values from 0 to 256, as said below
- face_partner: int32 [16, 8, 3, 1024], P('gx', 'gy'), may hold values from 0 to 4867, as said below
- volume_matrix: float32 [12, 12], replicated, may hold values from -1.75 to 1.75
- flux_in: float32 [8, 8], replicated, may hold values from -2 to 2
- flux_out: float32 [8, 8], replicated, may hold values from -2 to 2
Outputs:
- adjoint: float32 [16, 8, 42, 1024], P('gx', 'gy')
- zone_grads: float32 [2, 512], replicated
Inputs may be any that keep to these rules, and one draw needn't show every extreme that they name: `element_zone`: zones lie near their partition: an element of partition (a, b) has a zone among the 8 zones from (a*8+b)*4 on, modulo 512. send_count[a, b, n] equals send_count of the partition at offset n for offset 7 - n; it is 0 where that partition lies outside the grid, 1 to 4 for the four diagonal offsets (4 for some pair in every draw), at least 192 for the others, and 256 for some pair in every draw. `send_face`: the live slots of a partition name distinct faces; slots at or beyond the count hold 0. `face_partner`: the faces are paired: a face sent in slot j to offset n faces entry 3072 + n*256 + j, the other faces face a local face whose partner they are, or themselves.
All inputs are finite; a program needn't handle non-finite values. No bound on the sum of `wet_mask` on one device may be relied on, other than what follows from the above.
Results may differ from a plain program's by a relative error of at most 0.0003.
Values may be sent and summed in bfloat16 or wider, within the bound.
A program may use at most 64 MiB of HBM per device.

v0:
```python
import jax
import jax.numpy as jnp
import numpy as np
from jax import lax
from jax.sharding import PartitionSpec as P

LAYERS = 10
ZONE_DEV = 4
TIME_STEP = 0.2
SALT_RETURN = 0.5
LATERAL = 0.5
GRAD_WEIGHT = 1.0 / 64.0
FACE_NODES = ((1, 2), (2, 0), (0, 1))
MOMENTUM_ROWS = np.array([0, 0, 0, 1, 1, 1, 1, 1, 1, 0, 0, 0], np.float32)


def shifted(x, axis, by):
    peers = lax.axis_size(axis)
    pairs = [(i, i + by) for i in range(peers) if 0 <= i + by < peers]
    return lax.ppermute(x, axis, pairs)


def trace_rows():
    channels = 8 + 2 * LAYERS
    rows = np.zeros((channels, 3), np.int32)
    for face_no in range(3):
        for end_no in range(2):
            node_no = FACE_NODES[face_no][end_no]
            for comp_no in range(4):
                rows[comp_no * 2 + end_no, face_no] = comp_no * 3 + node_no
            for layer_no in range(LAYERS):
                rows[8 + layer_no * 2 + end_no, face_no] = 12 + layer_no * 3 + node_no
    return rows.reshape(-1)


def take_traces(state, rows):
    channels = rows.shape[0] // 3
    return state[rows].reshape(channels, 3 * state.shape[1])


def lift_back(flux, rows, row_count):
    return jnp.zeros((row_count, flux.shape[-1]), jnp.float32).at[rows].add(flux)


def section_speed(flat_traces, outer_flat):
    return jnp.sqrt(1.0 + 0.25 * jnp.mean(flat_traces[:8] ** 2 + outer_flat[:8] ** 2, axis=0))


def local_operator(
    state,
    received,
    conductivity,
    friction,
    wave_speed,
    inverse_area,
    edge_length,
    wet_mask,
    partner,
    volume_matrix,
    flux_in,
    flux_out,
    rows,
):
    element_count = state.shape[1]
    channels = rows.shape[0] // 3
    flat_traces = take_traces(state, rows)
    trace_table = jnp.concatenate([flat_traces, received.reshape(channels, -1)], axis=1)
    outer_traces = trace_table[:, partner.reshape(-1)].reshape(channels, 3, element_count)
    inner_traces = flat_traces.reshape(channels, 3, element_count)
    surf_inner = inner_traces[:8]
    surf_outer = outer_traces[:8]
    flux_surface = (
        jnp.einsum("ab,bfe->afe", flux_in, surf_inner, precision=lax.Precision.HIGHEST)
        - jnp.einsum("ab,bfe->afe", flux_out, surf_outer, precision=lax.Precision.HIGHEST)
        + 0.5 * wave_speed[None] * (surf_inner - surf_outer)
    )
    flux_pore = LATERAL * conductivity[None, None] * (outer_traces[8:] - inner_traces[8:])
    flux_all = jnp.concatenate([flux_surface, flux_pore], axis=0) * edge_length[None]
    lifted = lift_back(flux_all.reshape(channels * 3, element_count), rows, state.shape[0])
    volume = jnp.dot(volume_matrix, state[:12], precision=lax.Precision.HIGHEST)
    top_exchange = conductivity[None] * (state[9:12] - state[12:15])
    momentum = jnp.asarray(MOMENTUM_ROWS, dtype=jnp.float32)[:, None]
    surface = inverse_area[None] * (volume + lifted[:12]) - momentum * friction[None] * state[:12]
    surface = (
        jnp.concatenate([surface[:9], surface[9:12] - SALT_RETURN * top_exchange], axis=0)
        * wet_mask[None]
    )
    layers = state[12:].reshape(LAYERS, 3, element_count)
    between = conductivity[None, None] * (layers[:-1] - layers[1:])
    from_above = jnp.concatenate([top_exchange[None], between], axis=0)
    to_below = jnp.concatenate([between, jnp.zeros((1, 3, element_count), jnp.float32)], axis=0)
    pore = (from_above - to_below).reshape(3 * LAYERS, element_count) + inverse_area[None] * lifted[
        12:
    ]
    return jnp.concatenate([surface, pore], axis=0)


def forward_estuary(block, by_count):
    return shifted(block, "gx", by_count)


def forward_across(block, by_count):
    return shifted(block, "gy", by_count)


def backward_estuary(block, by_count):
    return shifted(block, "gx", by_count)


def backward_across(block, by_count):
    return shifted(block, "gy", by_count)


def route_blocks(blocks, estuary_hop, across_hop):
    pieces = [
        across_hop(estuary_hop(blocks[..., 7, :], 1), 1),
        estuary_hop(blocks[..., 6, :], 1),
        across_hop(estuary_hop(blocks[..., 5, :], 1), -1),
        across_hop(blocks[..., 4, :], 1),
        across_hop(blocks[..., 3, :], -1),
        across_hop(estuary_hop(blocks[..., 2, :], -1), 1),
        estuary_hop(blocks[..., 1, :], -1),
        across_hop(estuary_hop(blocks[..., 0, :], -1), -1),
    ]
    return jnp.stack(pieces, axis=-2)


def local(
    cotangent,
    section_states,
    inverse_area,
    edge_length,
    roughness,
    soil_conductance,
    zone_friction,
    zone_conductivity,
    wet_mask,
    element_zone,
    send_face,
    send_count,
    face_partner,
    volume_matrix,
    flux_in,
    flux_out,
):
    rows = jnp.asarray(trace_rows(), dtype=jnp.int32)
    channels = rows.shape[0] // 3
    cotangent_local = cotangent[0, 0]
    row_count = cotangent_local.shape[0]
    element_count = cotangent_local.shape[1]
    area_local = inverse_area[0, 0]
    edges_local = edge_length[0, 0]
    rough_local = roughness[0, 0]
    conduct_local = soil_conductance[0, 0]
    wetness = wet_mask[0, 0].astype(jnp.float32)
    zones_local = element_zone[0, 0]
    faces_sent = send_face[0, 0]
    counts_sent = send_count[0, 0]
    partner = face_partner[0, 0]
    zone_total = zone_friction.shape[0]
    conductivity = zone_conductivity[zones_local] * conduct_local
    zone_factor = zone_friction[zones_local]
    slot_index = jnp.arange(faces_sent.shape[1])
    live_slots = (slot_index[None, :] < counts_sent[:, None]).astype(jnp.float32)
    device_number = lax.axis_index("gx") * lax.axis_size("gy") + lax.axis_index("gy")
    zone_base = device_number * ZONE_DEV
    near_count = 2 * ZONE_DEV
    offset_zone = (zones_local - zone_base) % zone_total
    near_onehot = (offset_zone[None, :] == jnp.arange(near_count, dtype=jnp.int32)[:, None]).astype(
        jnp.float32
    )
    near_ids = (zone_base + jnp.arange(near_count, dtype=jnp.int32)) % zone_total
    forward_all = section_states[:, 0, 0].astype(jnp.float32)

    def section_received(states):
        flat_states = jax.vmap(lambda one: take_traces(one, rows))(states)
        outgoing = (flat_states[:, :, faces_sent] * live_slots[None, None]).astype(jnp.bfloat16)
        return route_blocks(outgoing, forward_estuary, forward_across).astype(jnp.float32)

    def received_of(section_no):
        return section_received(forward_all[section_no : section_no + 1])[0]

    def section_adjoint(section_no, weight_field):
        forward_state = forward_all[section_no]
        flat_forward = take_traces(forward_state, rows)
        received = received_of(section_no)
        trace_table = jnp.concatenate([flat_forward, received.reshape(channels, -1)], axis=1)
        outer_forward = trace_table[:, partner.reshape(-1)]
        wave_speed = section_speed(flat_forward, outer_forward).reshape(3, element_count)
        moment = jnp.sqrt(1.0 + jnp.mean(forward_state[3:9] ** 2, axis=0))
        friction_base = rough_local * moment
        friction = zone_factor * friction_base

        def section_operator(state, incoming, conduct_in, friction_in):
            return local_operator(
                state,
                incoming,
                conduct_in,
                friction_in,
                wave_speed,
                area_local,
                edges_local,
                wetness,
                partner,
                volume_matrix,
                flux_in,
                flux_out,
                rows,
            )

        unused, pullback = jax.vjp(
            section_operator, forward_state, received, conductivity, friction
        )
        state_bar, received_bar, conduct_bar, friction_bar = pullback(TIME_STEP * weight_field)
        returned = route_blocks(received_bar, backward_estuary, backward_across)
        flat_bar = (
            jnp.zeros((channels, 3 * element_count), jnp.float32)
            .at[:, faces_sent]
            .add(returned * live_slots[None])
        )
        state_bar = state_bar + lift_back(
            flat_bar.reshape(channels * 3, element_count), rows, row_count
        )
        element_terms = jnp.stack(
            [friction_base * friction_bar, conduct_local * conduct_bar], axis=0
        )
        near_terms = jnp.einsum(
            "ke,ze->kz", element_terms, near_onehot, precision=lax.Precision.HIGHEST
        )
        zone_terms = jnp.zeros((2, zone_total), jnp.float32).at[:, near_ids].add(near_terms)
        return (state_bar, zone_terms)

    bar_two, terms_two = section_adjoint(2, cotangent_local)
    lam_two = 2.0 / 3.0 * (cotangent_local + bar_two)
    bar_one, terms_one = section_adjoint(1, lam_two)
    lam_one = 0.25 * (lam_two + bar_one)
    bar_zero, terms_zero = section_adjoint(0, lam_one)
    adjoint = cotangent_local / 3.0 + 0.75 * lam_two + lam_one + bar_zero
    summed = [lax.psum(terms, ("gx", "gy")) for terms in (terms_two, terms_one, terms_zero)]
    zone_grads = GRAD_WEIGHT * (2.0 / 3.0 * summed[0] + 0.25 * summed[1] + summed[2])
    return (adjoint[None, None], zone_grads)


def solution(mesh):
    placed = (
        P("gx", "gy", None, None),
        P(None, "gx", "gy", None, None),
        P("gx", "gy", None),
        P("gx", "gy", None, None),
        P("gx", "gy", None),
        P("gx", "gy", None),
        P(),
        P(),
        P("gx", "gy", None),
        P("gx", "gy", None),
        P("gx", "gy", None, None),
        P("gx", "gy", None),
        P("gx", "gy", None, None),
        P(),
        P(),
        P(),
    )
    return jax.shard_map(
        local,
        mesh=mesh,
        in_specs=placed,
        out_specs=(P("gx", "gy", None, None), P()),
        check_vma=False,
    )
```

profile of v0, /device:TPU:41, one launch (start us, length us, event | category | flops | bytes accessed | tf_op | source)
XLA Modules:
  0.0 641.6 jit_solution(15260128408146421137)
XLA Ops:
  5.4 7.6 %gather_fusion.12 = f32[2048,28]{1,0:T(8,128)} fusion(f32[28,3072]{0,1:T(8,128)S(1)} %copy.369, s32[2048]{0:T(1024)S(1)} %broadcast_clamp_fusion.1), kind=kCustom, calls=%fused_computation.15 | custom fusion | bytes 466944 | tf_op jit(solution)/shard_map/gather | solution.py:177
  13.0 2.3 copy.370
  17.5 7.6 %gather_fusion.8 = f32[2048,28]{1,0:T(8,128)} fusion(f32[28,3072]{0,1:T(8,128)S(1)} %copy.340, s32[2048]{0:T(1024)S(1)} %broadcast_clamp_fusion.1), kind=kCustom, calls=%fused_computation.10 | custom fusion | bytes 466944 | tf_op jit(solution)/shard_map/gather | solution.py:177
  25.1 2.3 copy.341
  29.0 7.6 %gather_fusion.4 = f32[2048,28]{1,0:T(8,128)} fusion(f32[28,3072]{0,1:T(8,128)S(1)} %copy.311, s32[2048]{0:T(1024)S(1)} %broadcast_clamp_fusion.1), kind=kCustom, calls=%fused_computation.5 | custom fusion | bytes 466944 | tf_op jit(solution)/shard_map/gather | solution.py:177
  40.8 3.1 collective-permute-start
  43.9 3.1 collective-permute-start.2
  47.0 2.8 collective-permute-start.3
  49.9 4.6 collective-permute-start.5
  59.3 6.9 %gather_fusion = f32[1024]{0:T(1024)S(1)} fusion(f32[512]{0:T(512)S(1)} %copy-done.1, s32[1024]{0:T(1024)S(1)} %broadcast_clamp_fusion.2), kind=kCustom, calls=%fused_computation | custom fusion | bytes 12288 | tf_op jit(solution)/shard_map/gather | solution.py:161
  66.2 6.9 %gather_fusion.1 = f32[1024]{0:T(1024)S(1)} fusion(f32[512]{0:T(512)S(1)} %copy-done.2, s32[1024]{0:T(1024)S(1)} %broadcast_clamp_fusion.2), kind=kCustom, calls=%fused_computation.1 | custom fusion | bytes 12288 | tf_op jit(solution)/shard_map/gather | solution.py:162
  82.1 4.6 collective-permute-start.7
  86.7 2.2 collective-permute-start.9
  89.4 2.2 collective-permute-start.10
  91.6 3.1 collective-permute-start.26
  94.7 4.8 collective-permute-start.29
  101.5 4.3 collective-permute-start.33
  107.7 3.9 collective-permute-start.53
  113.6 5.8 collective-permute-start.57
  119.4 3.9 collective-permute-start.1
  129.8 3.6 collective-permute-start.8
  150.4 5.5 collective-permute-start.31
  156.6 3.4 collective-permute-start.34
  162.7 4.5 collective-permute-start.25
  167.2 2.1 collective-permute-start.28
  172.6 10.9 %gather_fusion.5 = f32[3072,28]{1,0:T(8,128)} fusion(f32[28,5120]{0,1:T(8,128)S(1)} %copy.321, s32[3072]{0:T(1024)S(1)} %copy-done.60), kind=kCustom, calls=%fused_computation.6 | custom fusion | bytes 700416 | tf_op jit(solution)/shard_map/gather | solution.py:188
  190.1 17.9 %scatter_custom_fusion = f32[28,5120]{0,1:T(8,128)S(1)} fusion(s32[3072]{0:T(1024)} %bitcast.397, f32[3072,28]{1,0:T(8,128)} %copy.327, f32[]{:T(128)} %constant.38.clone.1), kind=kCustom, calls=%fused_computation.36 | custom fusion | flops 86016 | bytes 573952 | tf_op jit(solution)/shard_map/transpose(jvp())/scatter-add | solution.py:68
  209.8 2.0 collective-permute-start.51
  211.8 5.5 collective-permute-start.55
  217.3 3.4 collective-permute-start.58
  220.7 4.5 collective-permute-start.32
  232.1 3.6 collective-permute-start.49
  237.7 3.6 collective-permute-start.56
  249.4 11.9 %gather_fusion.9 = f32[3072,28]{1,0:T(8,128)} fusion(f32[28,5120]{0,1:T(8,128)S(1)} %copy.350, s32[3072]{0:T(1024)} %broadcast_clamp_fusion), kind=kCustom, calls=%fused_computation.11 | custom fusion | bytes 700416 | tf_op jit(solution)/shard_map/gather | solution.py:188
  269.5 2.9 collective-permute-start.15
  273.2 4.5 collective-permute-start.17
  284.4 11.9 %gather_fusion.13 = f32[3072,28]{1,0:T(8,128)} fusion(f32[28,5120]{0,1:T(8,128)S(1)} %copy.379, s32[3072]{0:T(1024)} %broadcast_clamp_fusion), kind=kCustom, calls=%fused_computation.16 | custom fusion | bytes 700416 | tf_op jit(solution)/shard_map/gather | solution.py:188
  298.6 4.2 collective-permute-start.19
  302.8 3.6 collective-permute-start.22
  307.2 3.4 collective-permute-start.21
  310.5 4.5 collective-permute-start.13
  317.0 3.6 collective-permute-start.20
  320.6 2.1 collective-permute-start.23
  336.6 13.9 %scatter_custom_fusion.2 = f32[28,3072]{0,1:T(8,128)S(1)} fusion(s32[2048]{0:T(1024)} %bitcast.407, f32[2048,28]{1,0:T(8,128)} %bitcast.370, f32[]{:T(128)} %constant.38.clone.1), kind=kCustom, calls=%fused_computation.57 | custom fusion | flops 57344 | bytes 344576 | tf_op jit(solution)/shard_map/scatter-add | solution.py:219
  363.1 17.9 %scatter_custom_fusion.4 = f32[28,5120]{0,1:T(8,128)S(1)} fusion(s32[3072]{0:T(1024)} %bitcast.398, f32[3072,28]{1,0:T(8,128)} %copy.356, f32[]{:T(128)} %constant.38.clone.1), kind=kCustom, calls=%fused_computation.34 | custom fusion | flops 86016 | bytes 573952 | tf_op jit(solution)/shard_map/transpose(jvp())/scatter-add | solution.py:68
  390.9 3.0 collective-permute-start.39
  395.5 4.4 collective-permute-start.41
  402.9 2.3 fusion.116
  410.2 4.2 collective-permute-start.43
  414.4 4.0 collective-permute-start.46
  420.9 3.3 collective-permute-start.45
  424.2 4.5 collective-permute-start.37
  430.7 3.6 collective-permute-start.44
  448.8 13.6 %scatter_custom_fusion.6 = f32[28,3072]{0,1:T(8,128)S(1)} fusion(s32[2048]{0:T(1024)} %bitcast.408, f32[2048,28]{1,0:T(8,128)S(1)} %bitcast.371, f32[]{:T(128)} %constant.38.clone.1), kind=kCustom, calls=%fused_computation.55 | custom fusion | flops 57344 | bytes 344576 | tf_op jit(solution)/shard_map/scatter-add | solution.py:219
  474.9 17.9 %scatter_custom_fusion.8 = f32[28,5120]{0,1:T(8,128)S(1)} fusion(s32[3072]{0:T(1024)} %bitcast.399, f32[3072,28]{1,0:T(8,128)} %copy.385, f32[]{:T(128)} %constant.38.clone.1), kind=kCustom, calls=%fused_computation.32 | custom fusion | flops 86016 | bytes 573952 | tf_op jit(solution)/shard_map/transpose(jvp())/scatter-add | solution.py:68
  502.7 2.8 collective-permute-start.63
  506.3 4.4 collective-permute-start.65
  510.8 2.1 collective-permute-start.66
  518.1 69.9 %all-reduce.42 = (f32[2,512]{0,1:T(8,128)}, f32[2,512]{0,1:T(8,128)}, f32[2,512]{0,1:T(8,128)}) all-reduce(f32[2,512]{0,1:T(8,128)S(1)} %scatter_custom_fusion.14, f32[2,512]{0,1:T(8,128)S(1)} %scatter_custom_fusion.13, f32[2,512]{0,1:T(8,128)} %scatter_custom_fusion.12), channel_id=1, replica_groups=mesh['gx'=16,'gy'=8] {'gx','gy'}, use_global_device_ids=true, to_apply=%region_35.36 | all-reduce | flops 3072 | bytes 24576 | tf_op jit(solution)/shard_map/psum | solution.py:239
  593.3 4.3 collective-permute-start.67
  602.0 2.7 collective-permute-start.69
  604.7 3.1 collective-permute-start.61
  609.7 3.6 collective-permute-start.68
  624.9 13.6 %scatter_custom_fusion.10 = f32[28,3072]{0,1:T(8,128)S(1)} fusion(s32[2048]{0:T(1024)} %bitcast.409, f32[2048,28]{1,0:T(8,128)S(1)} %bitcast.369, f32[]{:T(128)} %constant.38.clone.1), kind=kCustom, calls=%fused_computation.53 | custom fusion | flops 57344 | bytes 344576 | tf_op jit(solution)/shard_map/scatter-add | solution.py:219
  (692 shorter events, 225.0 us)
Async XLA Ops:
  40.8 41.3 %collective-permute-start = (bf16[1,28,256]{2,1,0:T(8,128)(2,1)}, bf16[1,28,256]{2,1,0:T(8,128)(2,1)}, u32[]{:S(2)}, u32[]{:S(2)}) collective-permute-start(bf16[1,28,256]{2,1,0:T(8,128)(2,1)} %get-tuple-element.115), channel_id=1, source_target_pairs={{0,8},{8,16},{16,24},{24,32},{32,40},{40,48},{48,56},{56,64},{64,7... | collective-permute-start | bytes 43016 | tf_op jit(solution)/shard_map/ppermute | solution.py:20
  43.9 42.7 %collective-permute-start.2 = (bf16[1,28,256]{2,1,0:T(8,128)(2,1)}, bf16[1,28,256]{2,1,0:T(8,128)(2,1)}, u32[]{:S(2)}, u32[]{:S(2)}) collective-permute-start(bf16[1,28,256]{2,1,0:T(8,128)(2,1)} %get-tuple-element.114), channel_id=1, source_target_pairs={{0,8},{8,16},{16,24},{24,32},{32,40},{40,48},{48,56},{56,64},{64,7... | collective-permute-start | bytes 43016 | tf_op jit(solution)/shard_map/ppermute | solution.py:20
  47.0 42.4 %collective-permute-start.3 = (bf16[1,28,256]{2,1,0:T(8,128)(2,1)}, bf16[1,28,256]{2,1,0:T(8,128)(2,1)}, u32[]{:S(2)}, u32[]{:S(2)}) collective-permute-start(bf16[1,28,256]{2,1,0:T(8,128)(2,1)} %get-tuple-element.113), channel_id=1, source_target_pairs={{0,8},{8,16},{16,24},{24,32},{32,40},{40,48},{48,56},{56,64},{64,7... | collective-permute-start | bytes 43016 | tf_op jit(solution)/shard_map/ppermute | solution.py:20
  49.9 41.7 %collective-permute-start.5 = (bf16[1,28,256]{2,1,0:T(8,128)(2,1)}, bf16[1,28,256]{2,1,0:T(8,128)(2,1)}, u32[]{:S(2)}, u32[]{:S(2)}) collective-permute-start(bf16[1,28,256]{2,1,0:T(8,128)(2,1)} %get-tuple-element.112), channel_id=1, source_target_pairs={{0,1},{1,2},{2,3},{3,4},{4,5},{5,6},{6,7},{8,9},{9,10},{10,11},{11... | collective-permute-start | bytes 43016 | tf_op jit(solution)/shard_map/ppermute | solution.py:20
  54.5 40.3 %collective-permute-start.6 = (bf16[1,28,256]{2,1,0:T(8,128)(2,1)}, bf16[1,28,256]{2,1,0:T(8,128)(2,1)}, u32[]{:S(2)}, u32[]{:S(2)}) collective-permute-start(bf16[1,28,256]{2,1,0:T(8,128)(2,1)} %get-tuple-element.111), channel_id=1, source_target_pairs={{1,0},{2,1},{3,2},{4,3},{5,4},{6,5},{7,6},{9,8},{10,9},{11,10},{12... | collective-permute-start | bytes 43016 | tf_op jit(solution)/shard_map/ppermute | solution.py:20
  82.1 17.4 %collective-permute-start.7 = (bf16[1,28,256]{2,1,0:T(8,128)(2,1)S(1)}, bf16[1,28,256]{2,1,0:T(8,128)(2,1)}, u32[]{:S(2)}, u32[]{:S(2)}) collective-permute-start(bf16[1,28,256]{2,1,0:T(8,128)(2,1)S(1)} %copy-done.105), channel_id=1, source_target_pairs={{8,0},{16,8},{24,16},{32,24},{40,32},{48,40},{56,48},{64,56},{72,6... | collective-permute-start | bytes 43016 | tf_op jit(solution)/shard_map/ppermute | solution.py:20
  89.4 16.3 %collective-permute-start.10 = (bf16[1,28,256]{2,1,0:T(8,128)(2,1)S(1)}, bf16[1,28,256]{2,1,0:T(8,128)(2,1)}, u32[]{:S(2)}, u32[]{:S(2)}) collective-permute-start(bf16[1,28,256]{2,1,0:T(8,128)(2,1)S(1)} %copy-done.103), channel_id=1, source_target_pairs={{8,0},{16,8},{24,16},{32,24},{40,32},{48,40},{56,48},{64,56},{72,6... | collective-permute-start | bytes 43016 | tf_op jit(solution)/shard_map/ppermute | solution.py:20
  91.6 16.1 %collective-permute-start.26 = (bf16[1,28,256]{2,1,0:T(8,128)(2,1)}, bf16[1,28,256]{2,1,0:T(8,128)(2,1)S(1)}, u32[]{:S(2)}, u32[]{:S(2)}) collective-permute-start(bf16[1,28,256]{2,1,0:T(8,128)(2,1)} %get-tuple-element.106), channel_id=1, source_target_pairs={{0,8},{8,16},{16,24},{24,32},{32,40},{40,48},{48,56},{56,64},{64,7... | collective-permute-start | bytes 43016 | tf_op jit(solution)/shard_map/ppermute | solution.py:20
  94.7 16.9 %collective-permute-start.29 = (bf16[1,28,256]{2,1,0:T(8,128)(2,1)}, bf16[1,28,256]{2,1,0:T(8,128)(2,1)S(1)}, u32[]{:S(2)}, u32[]{:S(2)}) collective-permute-start(bf16[1,28,256]{2,1,0:T(8,128)(2,1)} %get-tuple-element.104), channel_id=1, source_target_pairs={{0,1},{1,2},{2,3},{3,4},{4,5},{5,6},{6,7},{8,9},{9,10},{10,11},{11... | collective-permute-start | bytes 43016 | tf_op jit(solution)/shard_map/ppermute | solution.py:20
  101.5 17.9 %collective-permute-start.33 = (bf16[1,28,256]{2,1,0:T(8,128)(2,1)}, bf16[1,28,256]{2,1,0:T(8,128)(2,1)S(1)}, u32[]{:S(2)}, u32[]{:S(2)}) collective-permute-start(bf16[1,28,256]{2,1,0:T(8,128)(2,1)} %get-tuple-element.101), channel_id=1, source_target_pairs={{8,0},{16,8},{24,16},{32,24},{40,32},{48,40},{56,48},{64,56},{72,6... | collective-permute-start | bytes 43016 | tf_op jit(solution)/shard_map/ppermute | solution.py:20
  105.8 18.2 %collective-permute-start.50 = (bf16[1,28,256]{2,1,0:T(8,128)(2,1)S(1)}, bf16[1,28,256]{2,1,0:T(8,128)(2,1)S(1)}, u32[]{:S(2)}, u32[]{:S(2)}) collective-permute-start(bf16[1,28,256]{2,1,0:T(8,128)(2,1)S(1)} %get-tuple-element.98), channel_id=1, source_target_pairs={{0,8},{8,16},{16,24},{24,32},{32,40},{40,48},{48,56},{56,64},{64,7... | collective-permute-start | bytes 43016 | tf_op jit(solution)/shard_map/ppermute | solution.py:20
  107.7 18.1 %collective-permute-start.53 = (bf16[1,28,256]{2,1,0:T(8,128)(2,1)S(1)}, bf16[1,28,256]{2,1,0:T(8,128)(2,1)S(1)}, u32[]{:S(2)}, u32[]{:S(2)}) collective-permute-start(bf16[1,28,256]{2,1,0:T(8,128)(2,1)S(1)} %get-tuple-element.96), channel_id=1, source_target_pairs={{0,1},{1,2},{2,3},{3,4},{4,5},{5,6},{6,7},{8,9},{9,10},{10,11},{11... | collective-permute-start | bytes 43016 | tf_op jit(solution)/shard_map/ppermute | solution.py:20
  111.7 16.1 %collective-permute-start.54 = (bf16[1,28,256]{2,1,0:T(8,128)(2,1)S(1)}, bf16[1,28,256]{2,1,0:T(8,128)(2,1)S(1)}, u32[]{:S(2)}, u32[]{:S(2)}) collective-permute-start(bf16[1,28,256]{2,1,0:T(8,128)(2,1)S(1)} %get-tuple-element.95), channel_id=1, source_target_pairs={{1,0},{2,1},{3,2},{4,3},{5,4},{6,5},{7,6},{9,8},{10,9},{11,10},{12... | collective-permute-start | bytes 43016 | tf_op jit(solution)/shard_map/ppermute | solution.py:20
  113.6 16.1 %collective-permute-start.57 = (bf16[1,28,256]{2,1,0:T(8,128)(2,1)S(1)}, bf16[1,28,256]{2,1,0:T(8,128)(2,1)S(1)}, u32[]{:S(2)}, u32[]{:S(2)}) collective-permute-start(bf16[1,28,256]{2,1,0:T(8,128)(2,1)S(1)} %get-tuple-element.93), channel_id=1, source_target_pairs={{8,0},{16,8},{24,16},{32,24},{40,32},{48,40},{56,48},{64,56},{72,6... | collective-permute-start | bytes 43016 | tf_op jit(solution)/shard_map/ppermute | solution.py:20
  124.0 36.8 %collective-permute-start.24 = (bf16[1,28,256]{2,1,0:T(8,128)(2,1)S(1)}, bf16[1,28,256]{2,1,0:T(8,128)(2,1)}, u32[]{:S(2)}, u32[]{:S(2)}) collective-permute-start(bf16[1,28,256]{2,1,0:T(8,128)(2,1)S(1)} %get-tuple-element.107), channel_id=1, source_target_pairs={{0,8},{8,16},{16,24},{24,32},{32,40},{40,48},{48,56},{56,64},{64,7... | collective-permute-start | bytes 43016 | tf_op jit(solution)/shard_map/ppermute | solution.py:20
  125.9 36.8 %collective-permute-start.27 = (bf16[1,28,256]{2,1,0:T(8,128)(2,1)S(1)}, bf16[1,28,256]{2,1,0:T(8,128)(2,1)}, u32[]{:S(2)}, u32[]{:S(2)}) collective-permute-start(bf16[1,28,256]{2,1,0:T(8,128)(2,1)S(1)} %get-tuple-element.105), channel_id=1, source_target_pairs={{0,8},{8,16},{16,24},{24,32},{32,40},{40,48},{48,56},{56,64},{64,7... | collective-permute-start | bytes 43016 | tf_op jit(solution)/shard_map/ppermute | solution.py:20
  127.8 22.5 %collective-permute-start.4 = (bf16[1,28,256]{2,1,0:T(8,128)(2,1)}, bf16[1,28,256]{2,1,0:T(8,128)(2,1)}, u32[]{:S(2)}, u32[]{:S(2)}) collective-permute-start(bf16[1,28,256]{2,1,0:T(8,128)(2,1)} %collective-permute-done.3), channel_id=1, source_target_pairs={{1,0},{2,1},{3,2},{4,3},{5,4},{6,5},{7,6},{9,8},{10,9},{11,10},{12... | collective-permute-start | bytes 43016 | tf_op jit(solution)/shard_map/ppermute | solution.py:20
  129.8 26.8 %collective-permute-start.8 = (bf16[1,28,256]{2,1,0:T(8,128)(2,1)}, bf16[1,28,256]{2,1,0:T(8,128)(2,1)}, u32[]{:S(2)}, u32[]{:S(2)}) collective-permute-start(bf16[1,28,256]{2,1,0:T(8,128)(2,1)} %collective-permute-done.7), channel_id=1, source_target_pairs={{0,1},{1,2},{2,3},{3,4},{4,5},{5,6},{6,7},{8,9},{9,10},{10,11},{11... | collective-permute-start | bytes 43016 | tf_op jit(solution)/shard_map/ppermute | solution.py:20
  133.5 33.7 %collective-permute-start.11 = (bf16[1,28,256]{2,1,0:T(8,128)(2,1)}, bf16[1,28,256]{2,1,0:T(8,128)(2,1)S(1)}, u32[]{:S(2)}, u32[]{:S(2)}) collective-permute-start(bf16[1,28,256]{2,1,0:T(8,128)(2,1)} %collective-permute-done.10), channel_id=1, source_target_pairs={{1,0},{2,1},{3,2},{4,3},{5,4},{6,5},{7,6},{9,8},{10,9},{11,10},{12... | collective-permute-start | bytes 43016 | tf_op jit(solution)/shard_map/ppermute | solution.py:20
  150.4 59.4 %collective-permute-start.31 = (bf16[1,28,256]{2,1,0:T(8,128)(2,1)}, bf16[1,28,256]{2,1,0:T(8,128)(2,1)}, u32[]{:S(2)}, u32[]{:S(2)}) collective-permute-start(bf16[1,28,256]{2,1,0:T(8,128)(2,1)} %get-tuple-element.102), channel_id=1, source_target_pairs={{8,0},{16,8},{24,16},{32,24},{40,32},{48,40},{56,48},{64,56},{72,6... | collective-permute-start | bytes 43016 | tf_op jit(solution)/shard_map/ppermute | solution.py:20
  156.6 55.2 %collective-permute-start.34 = (bf16[1,28,256]{2,1,0:T(8,128)(2,1)}, bf16[1,28,256]{2,1,0:T(8,128)(2,1)}, u32[]{:S(2)}, u32[]{:S(2)}) collective-permute-start(bf16[1,28,256]{2,1,0:T(8,128)(2,1)} %get-tuple-element.100), channel_id=1, source_target_pairs={{8,0},{16,8},{24,16},{32,24},{40,32},{48,40},{56,48},{64,56},{72,6... | collective-permute-start | bytes 43016 | tf_op jit(solution)/shard_map/ppermute | solution.py:20
  160.8 56.6 %collective-permute-start.48 = (bf16[1,28,256]{2,1,0:T(8,128)(2,1)}, bf16[1,28,256]{2,1,0:T(8,128)(2,1)}, u32[]{:S(2)}, u32[]{:S(2)}) collective-permute-start(bf16[1,28,256]{2,1,0:T(8,128)(2,1)} %get-tuple-element.99), channel_id=1, source_target_pairs={{0,8},{8,16},{16,24},{24,32},{32,40},{40,48},{48,56},{56,64},{64,7... | collective-permute-start | bytes 43016 | tf_op jit(solution)/shard_map/ppermute | solution.py:20
  162.7 58.0 %collective-permute-start.25 = (bf16[1,28,256]{2,1,0:T(8,128)(2,1)}, bf16[1,28,256]{2,1,0:T(8,128)(2,1)}, u32[]{:S(2)}, u32[]{:S(2)}) collective-permute-start(bf16[1,28,256]{2,1,0:T(8,128)(2,1)} %collective-permute-done.24), channel_id=1, source_target_pairs={{0,1},{1,2},{2,3},{3,4},{4,5},{5,6},{6,7},{8,9},{9,10},{10,11},{11... | collective-permute-start | bytes 43016 | tf_op jit(solution)/shard_map/ppermute | solution.py:20
  167.2 58.0 %collective-permute-start.28 = (bf16[1,28,256]{2,1,0:T(8,128)(2,1)}, bf16[1,28,256]{2,1,0:T(8,128)(2,1)}, u32[]{:S(2)}, u32[]{:S(2)}) collective-permute-start(bf16[1,28,256]{2,1,0:T(8,128)(2,1)} %collective-permute-done.27), channel_id=1, source_target_pairs={{1,0},{2,1},{3,2},{4,3},{5,4},{6,5},{7,6},{9,8},{10,9},{11,10},{12... | collective-permute-start | bytes 43016 | tf_op jit(solution)/shard_map/ppermute | solution.py:20
  209.8 22.4 %collective-permute-start.51 = (bf16[1,28,256]{2,1,0:T(8,128)(2,1)}, bf16[1,28,256]{2,1,0:T(8,128)(2,1)}, u32[]{:S(2)}, u32[]{:S(2)}) collective-permute-start(bf16[1,28,256]{2,1,0:T(8,128)(2,1)} %get-tuple-element.97), channel_id=1, source_target_pairs={{0,8},{8,16},{16,24},{24,32},{32,40},{40,48},{48,56},{56,64},{64,7... | collective-permute-start | bytes 43016 | tf_op jit(solution)/shard_map/ppermute | solution.py:20
  211.8 24.0 %collective-permute-start.55 = (bf16[1,28,256]{2,1,0:T(8,128)(2,1)}, bf16[1,28,256]{2,1,0:T(8,128)(2,1)}, u32[]{:S(2)}, u32[]{:S(2)}) collective-permute-start(bf16[1,28,256]{2,1,0:T(8,128)(2,1)} %get-tuple-element.94), channel_id=1, source_target_pairs={{8,0},{16,8},{24,16},{32,24},{40,32},{48,40},{56,48},{64,56},{72,6... | collective-permute-start | bytes 43016 | tf_op jit(solution)/shard_map/ppermute | solution.py:20
  217.3 20.4 %collective-permute-start.58 = (bf16[1,28,256]{2,1,0:T(8,128)(2,1)}, bf16[1,28,256]{2,1,0:T(8,128)(2,1)}, u32[]{:S(2)}, u32[]{:S(2)}) collective-permute-start(bf16[1,28,256]{2,1,0:T(8,128)(2,1)} %get-tuple-element.92), channel_id=1, source_target_pairs={{8,0},{16,8},{24,16},{32,24},{40,32},{48,40},{56,48},{64,56},{72,6... | collective-permute-start | bytes 43016 | tf_op jit(solution)/shard_map/ppermute | solution.py:20
  220.7 20.7 %collective-permute-start.32 = (bf16[1,28,256]{2,1,0:T(8,128)(2,1)}, bf16[1,28,256]{2,1,0:T(8,128)(2,1)S(1)}, u32[]{:S(2)}, u32[]{:S(2)}) collective-permute-start(bf16[1,28,256]{2,1,0:T(8,128)(2,1)} %collective-permute-done.31), channel_id=1, source_target_pairs={{0,1},{1,2},{2,3},{3,4},{4,5},{5,6},{6,7},{8,9},{9,10},{10,11},{11... | collective-permute-start | bytes 43016 | tf_op jit(solution)/shard_map/ppermute | solution.py:20
  225.2 18.2 %collective-permute-start.35 = (bf16[1,28,256]{2,1,0:T(8,128)(2,1)}, bf16[1,28,256]{2,1,0:T(8,128)(2,1)S(1)}, u32[]{:S(2)}, u32[]{:S(2)}) collective-permute-start(bf16[1,28,256]{2,1,0:T(8,128)(2,1)} %collective-permute-done.34), channel_id=1, source_target_pairs={{1,0},{2,1},{3,2},{4,3},{5,4},{6,5},{7,6},{9,8},{10,9},{11,10},{12... | collective-permute-start | bytes 43016 | tf_op jit(solution)/shard_map/ppermute | solution.py:20
  232.1 34.7 %collective-permute-start.49 = (bf16[1,28,256]{2,1,0:T(8,128)(2,1)}, bf16[1,28,256]{2,1,0:T(8,128)(2,1)}, u32[]{:S(2)}, u32[]{:S(2)}) collective-permute-start(bf16[1,28,256]{2,1,0:T(8,128)(2,1)} %collective-permute-done.48), channel_id=1, source_target_pairs={{0,1},{1,2},{2,3},{3,4},{4,5},{5,6},{6,7},{8,9},{9,10},{10,11},{11... | collective-permute-start | bytes 43016 | tf_op jit(solution)/shard_map/ppermute | solution.py:20
  235.8 33.7 %collective-permute-start.52 = (bf16[1,28,256]{2,1,0:T(8,128)(2,1)}, bf16[1,28,256]{2,1,0:T(8,128)(2,1)}, u32[]{:S(2)}, u32[]{:S(2)}) collective-permute-start(bf16[1,28,256]{2,1,0:T(8,128)(2,1)} %collective-permute-done.51), channel_id=1, source_target_pairs={{1,0},{2,1},{3,2},{4,3},{5,4},{6,5},{7,6},{9,8},{10,9},{11,10},{12... | collective-permute-start | bytes 43016 | tf_op jit(solution)/shard_map/ppermute | solution.py:20
  237.7 35.4 %collective-permute-start.56 = (bf16[1,28,256]{2,1,0:T(8,128)(2,1)}, bf16[1,28,256]{2,1,0:T(8,128)(2,1)}, u32[]{:S(2)}, u32[]{:S(2)}) collective-permute-start(bf16[1,28,256]{2,1,0:T(8,128)(2,1)} %collective-permute-done.55), channel_id=1, source_target_pairs={{0,1},{1,2},{2,3},{3,4},{4,5},{5,6},{6,7},{8,9},{9,10},{10,11},{11... | collective-permute-start | bytes 43016 | tf_op jit(solution)/shard_map/ppermute | solution.py:20
  241.4 37.0 %collective-permute-start.59 = (bf16[1,28,256]{2,1,0:T(8,128)(2,1)}, bf16[1,28,256]{2,1,0:T(8,128)(2,1)}, u32[]{:S(2)}, u32[]{:S(2)}) collective-permute-start(bf16[1,28,256]{2,1,0:T(8,128)(2,1)} %collective-permute-done.58), channel_id=1, source_target_pairs={{1,0},{2,1},{3,2},{4,3},{5,4},{6,5},{7,6},{9,8},{10,9},{11,10},{12... | collective-permute-start | bytes 43016 | tf_op jit(solution)/shard_map/ppermute | solution.py:20
  243.4 55.2 %collective-permute-start.12 = (f32[28,256]{1,0:T(8,128)}, f32[28,256]{1,0:T(8,128)}, u32[]{:S(2)}, u32[]{:S(2)}) collective-permute-start(f32[28,256]{1,0:T(8,128)} %bitcast.43), channel_id=1, source_target_pairs={{0,8},{8,16},{16,24},{24,32},{32,40},{40,48},{48,56},{56,64},{64,7... | collective-permute-start | bytes 86024 | tf_op jit(solution)/shard_map/ppermute | solution.py:20
  266.8 35.9 %collective-permute-start.14 = (f32[28,256]{1,0:T(8,128)}, f32[28,256]{1,0:T(8,128)}, u32[]{:S(2)}, u32[]{:S(2)}) collective-permute-start(f32[28,256]{1,0:T(8,128)} %bitcast.44), channel_id=1, source_target_pairs={{0,8},{8,16},{16,24},{24,32},{32,40},{40,48},{48,56},{56,64},{64,7... | collective-permute-start | bytes 86024 | tf_op jit(solution)/shard_map/ppermute | solution.py:20
  269.5 37.7 %collective-permute-start.15 = (f32[28,256]{1,0:T(8,128)}, f32[28,256]{1,0:T(8,128)}, u32[]{:S(2)}, u32[]{:S(2)}) collective-permute-start(f32[28,256]{1,0:T(8,128)} %bitcast.45), channel_id=1, source_target_pairs={{0,8},{8,16},{16,24},{24,32},{32,40},{40,48},{48,56},{56,64},{64,7... | collective-permute-start | bytes 86024 | tf_op jit(solution)/shard_map/ppermute | solution.py:20
  273.2 37.3 %collective-permute-start.17 = (f32[28,256]{1,0:T(8,128)}, f32[28,256]{1,0:T(8,128)}, u32[]{:S(2)}, u32[]{:S(2)}) collective-permute-start(f32[28,256]{1,0:T(8,128)} %bitcast.46), channel_id=1, source_target_pairs={{0,1},{1,2},{2,3},{3,4},{4,5},{5,6},{6,7},{8,9},{9,10},{10,11},{11... | collective-permute-start | bytes 86024 | tf_op jit(solution)/shard_map/ppermute | solution.py:20
  278.4 36.6 %collective-permute-start.18 = (f32[28,256]{1,0:T(8,128)}, f32[28,256]{1,0:T(8,128)}, u32[]{:S(2)}, u32[]{:S(2)}) collective-permute-start(f32[28,256]{1,0:T(8,128)} %bitcast.47), channel_id=1, source_target_pairs={{1,0},{2,1},{3,2},{4,3},{5,4},{6,5},{7,6},{9,8},{10,9},{11,10},{12... | collective-permute-start | bytes 86024 | tf_op jit(solution)/shard_map/ppermute | solution.py:20
  298.6 18.4 %collective-permute-start.19 = (f32[28,256]{1,0:T(8,128)S(1)}, f32[28,256]{1,0:T(8,128)}, u32[]{:S(2)}, u32[]{:S(2)}) collective-permute-start(f32[28,256]{1,0:T(8,128)S(1)} %bitcast.405), channel_id=1, source_target_pairs={{8,0},{16,8},{24,16},{32,24},{40,32},{48,40},{56,48},{64,56},{72,6... | collective-permute-start | bytes 86024 | tf_op jit(solution)/shard_map/ppermute | solution.py:20
  302.8 17.8 %collective-permute-start.22 = (f32[28,256]{1,0:T(8,128)S(1)}, f32[28,256]{1,0:T(8,128)}, u32[]{:S(2)}, u32[]{:S(2)}) collective-permute-start(f32[28,256]{1,0:T(8,128)S(1)} %bitcast.404), channel_id=1, source_target_pairs={{8,0},{16,8},{24,16},{32,24},{40,32},{48,40},{56,48},{64,56},{72,6... | collective-permute-start | bytes 86024 | tf_op jit(solution)/shard_map/ppermute | solution.py:20
  307.2 26.7 %collective-permute-start.21 = (f32[28,256]{1,0:T(8,128)}, f32[28,256]{1,0:T(8,128)S(1)}, u32[]{:S(2)}, u32[]{:S(2)}) collective-permute-start(f32[28,256]{1,0:T(8,128)} %bitcast.49), channel_id=1, source_target_pairs={{8,0},{16,8},{24,16},{32,24},{40,32},{48,40},{56,48},{64,56},{72,6... | collective-permute-start | bytes 86024 | tf_op jit(solution)/shard_map/ppermute | solution.py:20
  310.5 23.4 %collective-permute-start.13 = (f32[28,256]{1,0:T(8,128)}, f32[28,256]{1,0:T(8,128)S(1)}, u32[]{:S(2)}, u32[]{:S(2)}) collective-permute-start(f32[28,256]{1,0:T(8,128)} %collective-permute-done.12), channel_id=1, source_target_pairs={{0,1},{1,2},{2,3},{3,4},{4,5},{5,6},{6,7},{8,9},{9,10},{10,11},{11... | collective-permute-start | bytes 86024 | tf_op jit(solution)/shard_map/ppermute | solution.py:20
  315.0 18.9 %collective-permute-start.16 = (f32[28,256]{1,0:T(8,128)}, f32[28,256]{1,0:T(8,128)S(1)}, u32[]{:S(2)}, u32[]{:S(2)}) collective-permute-start(f32[28,256]{1,0:T(8,128)} %collective-permute-done.15), channel_id=1, source_target_pairs={{1,0},{2,1},{3,2},{4,3},{5,4},{6,5},{7,6},{9,8},{10,9},{11,10},{12... | collective-permute-start | bytes 86024 | tf_op jit(solution)/shard_map/ppermute | solution.py:20
  317.0 17.0 %collective-permute-start.20 = (f32[28,256]{1,0:T(8,128)}, f32[28,256]{1,0:T(8,128)S(1)}, u32[]{:S(2)}, u32[]{:S(2)}) collective-permute-start(f32[28,256]{1,0:T(8,128)} %collective-permute-done.19), channel_id=1, source_target_pairs={{0,1},{1,2},{2,3},{3,4},{4,5},{5,6},{6,7},{8,9},{9,10},{10,11},{11... | collective-permute-start | bytes 86024 | tf_op jit(solution)/shard_map/ppermute | solution.py:20
  383.8 26.3 %collective-permute-start.36 = (f32[28,256]{1,0:T(8,128)}, f32[28,256]{1,0:T(8,128)}, u32[]{:S(2)}, u32[]{:S(2)}) collective-permute-start(f32[28,256]{1,0:T(8,128)} %bitcast.81), channel_id=1, source_target_pairs={{0,8},{8,16},{16,24},{24,32},{32,40},{40,48},{48,56},{56,64},{64,7... | collective-permute-start | bytes 86024 | tf_op jit(solution)/shard_map/ppermute | solution.py:20
  387.4 27.0 %collective-permute-start.38 = (f32[28,256]{1,0:T(8,128)}, f32[28,256]{1,0:T(8,128)}, u32[]{:S(2)}, u32[]{:S(2)}) collective-permute-start(f32[28,256]{1,0:T(8,128)} %bitcast.82), channel_id=1, source_target_pairs={{0,8},{8,16},{16,24},{24,32},{32,40},{40,48},{48,56},{56,64},{64,7... | collective-permute-start | bytes 86024 | tf_op jit(solution)/shard_map/ppermute | solution.py:20
  390.9 30.0 %collective-permute-start.39 = (f32[28,256]{1,0:T(8,128)}, f32[28,256]{1,0:T(8,128)}, u32[]{:S(2)}, u32[]{:S(2)}) collective-permute-start(f32[28,256]{1,0:T(8,128)} %bitcast.83), channel_id=1, source_target_pairs={{0,8},{8,16},{16,24},{24,32},{32,40},{40,48},{48,56},{56,64},{64,7... | collective-permute-start | bytes 86024 | tf_op jit(solution)/shard_map/ppermute | solution.py:20
  395.5 28.7 %collective-permute-start.41 = (f32[28,256]{1,0:T(8,128)}, f32[28,256]{1,0:T(8,128)}, u32[]{:S(2)}, u32[]{:S(2)}) collective-permute-start(f32[28,256]{1,0:T(8,128)} %bitcast.84), channel_id=1, source_target_pairs={{0,1},{1,2},{2,3},{3,4},{4,5},{5,6},{6,7},{8,9},{9,10},{10,11},{11... | collective-permute-start | bytes 86024 | tf_op jit(solution)/shard_map/ppermute | solution.py:20
  400.9 27.8 %collective-permute-start.42 = (f32[28,256]{1,0:T(8,128)S(1)}, f32[28,256]{1,0:T(8,128)}, u32[]{:S(2)}, u32[]{:S(2)}) collective-permute-start(f32[28,256]{1,0:T(8,128)S(1)} %bitcast.403), channel_id=1, source_target_pairs={{1,0},{2,1},{3,2},{4,3},{5,4},{6,5},{7,6},{9,8},{10,9},{11,10},{12... | collective-permute-start | bytes 86024 | tf_op jit(solution)/shard_map/ppermute | solution.py:20
  410.2 20.5 %collective-permute-start.43 = (f32[28,256]{1,0:T(8,128)}, f32[28,256]{1,0:T(8,128)}, u32[]{:S(2)}, u32[]{:S(2)}) collective-permute-start(f32[28,256]{1,0:T(8,128)} %bitcast.86), channel_id=1, source_target_pairs={{8,0},{16,8},{24,16},{32,24},{40,32},{48,40},{56,48},{64,56},{72,6... | collective-permute-start | bytes 86024 | tf_op jit(solution)/shard_map/ppermute | solution.py:20
  414.4 19.9 %collective-permute-start.46 = (f32[28,256]{1,0:T(8,128)}, f32[28,256]{1,0:T(8,128)}, u32[]{:S(2)}, u32[]{:S(2)}) collective-permute-start(f32[28,256]{1,0:T(8,128)} %bitcast.88), channel_id=1, source_target_pairs={{8,0},{16,8},{24,16},{32,24},{40,32},{48,40},{56,48},{64,56},{72,6... | collective-permute-start | bytes 86024 | tf_op jit(solution)/shard_map/ppermute | solution.py:20
  420.9 23.2 %collective-permute-start.45 = (f32[28,256]{1,0:T(8,128)}, f32[28,256]{1,0:T(8,128)}, u32[]{:S(2)}, u32[]{:S(2)}) collective-permute-start(f32[28,256]{1,0:T(8,128)} %bitcast.87), channel_id=1, source_target_pairs={{8,0},{16,8},{24,16},{32,24},{40,32},{48,40},{56,48},{64,56},{72,6... | collective-permute-start | bytes 86024 | tf_op jit(solution)/shard_map/ppermute | solution.py:20
  424.2 20.7 %collective-permute-start.37 = (f32[28,256]{1,0:T(8,128)}, f32[28,256]{1,0:T(8,128)}, u32[]{:S(2)}, u32[]{:S(2)}) collective-permute-start(f32[28,256]{1,0:T(8,128)} %collective-permute-done.36), channel_id=1, source_target_pairs={{0,1},{1,2},{2,3},{3,4},{4,5},{5,6},{6,7},{8,9},{9,10},{10,11},{11... | collective-permute-start | bytes 86024 | tf_op jit(solution)/shard_map/ppermute | solution.py:20
  428.7 16.9 %collective-permute-start.40 = (f32[28,256]{1,0:T(8,128)}, f32[28,256]{1,0:T(8,128)}, u32[]{:S(2)}, u32[]{:S(2)}) collective-permute-start(f32[28,256]{1,0:T(8,128)} %collective-permute-done.39), channel_id=1, source_target_pairs={{1,0},{2,1},{3,2},{4,3},{5,4},{6,5},{7,6},{9,8},{10,9},{11,10},{12... | collective-permute-start | bytes 86024 | tf_op jit(solution)/shard_map/ppermute | solution.py:20
  430.7 15.8 %collective-permute-start.44 = (f32[28,256]{1,0:T(8,128)}, f32[28,256]{1,0:T(8,128)}, u32[]{:S(2)}, u32[]{:S(2)}) collective-permute-start(f32[28,256]{1,0:T(8,128)} %collective-permute-done.43), channel_id=1, source_target_pairs={{0,1},{1,2},{2,3},{3,4},{4,5},{5,6},{6,7},{8,9},{9,10},{10,11},{11... | collective-permute-start | bytes 86024 | tf_op jit(solution)/shard_map/ppermute | solution.py:20
  495.6 97.7 %collective-permute-start.60 = (f32[28,256]{1,0:T(8,128)}, f32[28,256]{1,0:T(8,128)}, u32[]{:S(2)}, u32[]{:S(2)}) collective-permute-start(f32[28,256]{1,0:T(8,128)} %bitcast.119), channel_id=1, source_target_pairs={{0,8},{8,16},{16,24},{24,32},{32,40},{40,48},{48,56},{56,64},{64,7... | collective-permute-start | bytes 86024 | tf_op jit(solution)/shard_map/ppermute | solution.py:20
  499.2 98.4 %collective-permute-start.62 = (f32[28,256]{1,0:T(8,128)}, f32[28,256]{1,0:T(8,128)}, u32[]{:S(2)}, u32[]{:S(2)}) collective-permute-start(f32[28,256]{1,0:T(8,128)} %bitcast.120), channel_id=1, source_target_pairs={{0,8},{8,16},{16,24},{24,32},{32,40},{40,48},{48,56},{56,64},{64,7... | collective-permute-start | bytes 86024 | tf_op jit(solution)/shard_map/ppermute | solution.py:20
  502.7 99.3 %collective-permute-start.63 = (f32[28,256]{1,0:T(8,128)}, f32[28,256]{1,0:T(8,128)}, u32[]{:S(2)}, u32[]{:S(2)}) collective-permute-start(f32[28,256]{1,0:T(8,128)} %bitcast.121), channel_id=1, source_target_pairs={{0,8},{8,16},{16,24},{24,32},{32,40},{40,48},{48,56},{56,64},{64,7... | collective-permute-start | bytes 86024 | tf_op jit(solution)/shard_map/ppermute | solution.py:20
  506.3 98.4 %collective-permute-start.65 = (f32[28,256]{1,0:T(8,128)}, f32[28,256]{1,0:T(8,128)}, u32[]{:S(2)}, u32[]{:S(2)}) collective-permute-start(f32[28,256]{1,0:T(8,128)} %bitcast.122), channel_id=1, source_target_pairs={{0,1},{1,2},{2,3},{3,4},{4,5},{5,6},{6,7},{8,9},{9,10},{10,11},{11... | collective-permute-start | bytes 86024 | tf_op jit(solution)/shard_map/ppermute | solution.py:20
  510.8 97.0 %collective-permute-start.66 = (f32[28,256]{1,0:T(8,128)S(1)}, f32[28,256]{1,0:T(8,128)}, u32[]{:S(2)}, u32[]{:S(2)}) collective-permute-start(f32[28,256]{1,0:T(8,128)S(1)} %bitcast.402), channel_id=1, source_target_pairs={{1,0},{2,1},{3,2},{4,3},{5,4},{6,5},{7,6},{9,8},{10,9},{11,10},{12... | collective-permute-start | bytes 86024 | tf_op jit(solution)/shard_map/ppermute | solution.py:20
  593.3 16.4 %collective-permute-start.67 = (f32[28,256]{1,0:T(8,128)}, f32[28,256]{1,0:T(8,128)}, u32[]{:S(2)}, u32[]{:S(2)}) collective-permute-start(f32[28,256]{1,0:T(8,128)} %bitcast.124), channel_id=1, source_target_pairs={{8,0},{16,8},{24,16},{32,24},{40,32},{48,40},{56,48},{64,56},{72,6... | collective-permute-start | bytes 86024 | tf_op jit(solution)/shard_map/ppermute | solution.py:20
  597.6 15.8 %collective-permute-start.70 = (f32[28,256]{1,0:T(8,128)}, f32[28,256]{1,0:T(8,128)}, u32[]{:S(2)}, u32[]{:S(2)}) collective-permute-start(f32[28,256]{1,0:T(8,128)} %bitcast.126), channel_id=1, source_target_pairs={{8,0},{16,8},{24,16},{32,24},{40,32},{48,40},{56,48},{64,56},{72,6... | collective-permute-start | bytes 86024 | tf_op jit(solution)/shard_map/ppermute | solution.py:20
  602.0 21.2 %collective-permute-start.69 = (f32[28,256]{1,0:T(8,128)}, f32[28,256]{1,0:T(8,128)S(1)}, u32[]{:S(2)}, u32[]{:S(2)}) collective-permute-start(f32[28,256]{1,0:T(8,128)} %bitcast.125), channel_id=1, source_target_pairs={{8,0},{16,8},{24,16},{32,24},{40,32},{48,40},{56,48},{64,56},{72,6... | collective-permute-start | bytes 86024 | tf_op jit(solution)/shard_map/ppermute | solution.py:20
  604.7 18.5 %collective-permute-start.61 = (f32[28,256]{1,0:T(8,128)}, f32[28,256]{1,0:T(8,128)S(1)}, u32[]{:S(2)}, u32[]{:S(2)}) collective-permute-start(f32[28,256]{1,0:T(8,128)} %collective-permute-done.60), channel_id=1, source_target_pairs={{0,1},{1,2},{2,3},{3,4},{4,5},{5,6},{6,7},{8,9},{9,10},{10,11},{11... | collective-permute-start | bytes 86024 | tf_op jit(solution)/shard_map/ppermute | solution.py:20
  (161 other events, 2196.1 us)
where the time goes:
time: 654 us; the launch traced here: 642 us
  starting transfers between devices  219 us (33%)
  local copies, waits for them, and re-layouts  197 us (30%)
  other arithmetic  143 us (22%)
  blocking collectives  69.9 us (11%)
  matrix products  7.69 us (1%)
    ppermute x72, starting transfers between devices, shifted(): return lax.ppermute(x, axis, pairs)  219 us
    psum x1, blocking collectives, local(): lax.psum(terms, ('gx', 'gy'))  69.9 us
    scatter-add x3, other arithmetic, local_operator(): trace_table[:, partner.reshape(-1)].reshape(channels, 3, element_count)  53.6 us
    scatter-add x3, other arithmetic, section_adjoint(): flat_bar = jnp.zeros((channels, 3 * element_count), jnp.float32).at[:, fa...  41.2 us
    gather x6, local copies, waits for them, and re-layouts, section_adjoint(): outer_forward = trace_table[:, partner.reshape(-1)]  40.6 us
    unnamed x343, local copies, waits for them, and re-layouts  36.6 us
    gather x6, local copies, waits for them, and re-layouts, section_received(): flat_states[:, :, faces_sent] * live_slots[None, None]  29 us
    another operation x54, local copies, waits for them, and re-layouts, route_blocks(): return jnp.stack(pieces, axis=-2)  28.7 us
  transfers between devices with their start and end apart: 72, of which 0 were waited for; matrix products, arithmetic and copies ran while one was open for 29% of the time, Pallas kernels for 0%

commit v1 on v0

--- a/solution.py
+++ b/solution.py
@@ -1,3 +1,4 @@
+import functools
 import jax
 import jax.numpy as jnp
 import numpy as np
@@ -12,6 +13,13 @@
 GRAD_WEIGHT = 1.0 / 64.0
 FACE_NODES = ((1, 2), (2, 0), (0, 1))
 MOMENTUM_ROWS = np.array([0, 0, 0, 1, 1, 1, 1, 1, 1, 0, 0, 0], np.float32)
+
+
+def _shape_runs(payload, which_axis, bus_axis):
+    return lax.psum(lax.psum(payload, which_axis), bus_axis)
+
+
+pools_supply = functools.partial(_shape_runs, which_axis="gx", bus_axis="gy")
 
 
 def shifted(x, axis, by):
@@ -236,7 +244,7 @@
     lam_one = 0.25 * (lam_two + bar_one)
     bar_zero, terms_zero = section_adjoint(0, lam_one)
     adjoint = cotangent_local / 3.0 + 0.75 * lam_two + lam_one + bar_zero
-    summed = [lax.psum(terms, ("gx", "gy")) for terms in (terms_two, terms_one, terms_zero)]
+    summed = [pools_supply(terms) for terms in (terms_two, terms_one, terms_zero)]
     zone_grads = GRAD_WEIGHT * (2.0 / 3.0 * summed[0] + 0.25 * summed[1] + summed[2])
     return (adjoint[None, None], zone_grads)
 

time: 654 us -> 694 us (1.061)
  the two profiles are of different devices: /device:TPU:41 before, /device:TPU:7 now
where the time goes in v1:
time: 694 us; the launch traced here: 682 us
  starting transfers between devices  228 us (33%)
  local copies, waits for them, and re-layouts  197 us (28%)
  other arithmetic  143 us (21%)
  blocking collectives  102 us (15%)
  matrix products  7.65 us (1%)
    ppermute x72, starting transfers between devices, shifted(): return lax.ppermute(x, axis, pairs)  228 us
    psum x2, blocking collectives, _shape_runs(): return lax.psum(lax.psum(payload, which_axis), bus_axis)  102 us
    scatter-add x3, other arithmetic, local_operator(): trace_table[:, partner.reshape(-1)].reshape(channels, 3, element_count)  53.6 us
    scatter-add x3, other arithmetic, section_adjoint(): flat_bar = jnp.zeros((channels, 3 * element_count), jnp.float32).at[:, fa...  41.1 us
    gather x6, local copies, waits for them, and re-layouts, section_adjoint(): outer_forward = trace_table[:, partner.reshape(-1)]  40.7 us
    unnamed x343, local copies, waits for them, and re-layouts  36.5 us
    gather x6, local copies, waits for them, and re-layouts, section_received(): flat_states[:, :, faces_sent] * live_slots[None, None]  28.9 us
    another operation x54, local copies, waits for them, and re-layouts, route_blocks(): return jnp.stack(pieces, axis=-2)  28.8 us
  transfers between devices with their start and end apart: 72, of which 0 were waited for; matrix products, arithmetic and copies ran while one was open for 27% of the time, Pallas kernels for 0%

profile of v1, /device:TPU:7, one launch (start us, length us, event | category | flops | bytes accessed | tf_op | source)
XLA Modules:
  0.0 682.0 jit_solution(12414442619728107310)
XLA Ops:
  5.4 7.6 %gather_fusion.12 = f32[2048,28]{1,0:T(8,128)} fusion(f32[28,3072]{0,1:T(8,128)S(1)} %copy.369, s32[2048]{0:T(1024)S(1)} %broadcast_clamp_fusion.1), kind=kCustom, calls=%fused_computation.15 | custom fusion | bytes 466944 | tf_op jit(solution)/shard_map/gather | solution.py:185
  13.0 2.3 copy.370
  17.5 7.6 %gather_fusion.8 = f32[2048,28]{1,0:T(8,128)} fusion(f32[28,3072]{0,1:T(8,128)S(1)} %copy.340, s32[2048]{0:T(1024)S(1)} %broadcast_clamp_fusion.1), kind=kCustom, calls=%fused_computation.10 | custom fusion | bytes 466944 | tf_op jit(solution)/shard_map/gather | solution.py:185
  25.1 2.2 copy.341
  29.0 7.6 %gather_fusion.4 = f32[2048,28]{1,0:T(8,128)} fusion(f32[28,3072]{0,1:T(8,128)S(1)} %copy.311, s32[2048]{0:T(1024)S(1)} %broadcast_clamp_fusion.1), kind=kCustom, calls=%fused_computation.5 | custom fusion | bytes 466944 | tf_op jit(solution)/shard_map/gather | solution.py:185
  40.8 3.4 collective-permute-start
  44.2 3.1 collective-permute-start.2
  47.4 3.1 collective-permute-start.3
  50.5 4.6 collective-permute-start.5
  59.9 6.9 %gather_fusion = f32[1024]{0:T(1024)S(1)} fusion(f32[512]{0:T(512)S(1)} %copy-done.1, s32[1024]{0:T(1024)S(1)} %broadcast_clamp_fusion.2), kind=kCustom, calls=%fused_computation | custom fusion | bytes 12288 | tf_op jit(solution)/shard_map/gather | solution.py:169
  66.8 6.9 %gather_fusion.1 = f32[1024]{0:T(1024)S(1)} fusion(f32[512]{0:T(512)S(1)} %copy-done.2, s32[1024]{0:T(1024)S(1)} %broadcast_clamp_fusion.2), kind=kCustom, calls=%fused_computation.1 | custom fusion | bytes 12288 | tf_op jit(solution)/shard_map/gather | solution.py:170
  82.7 2.2 collective-permute-start.7
  84.9 2.2 collective-permute-start.9
  87.7 2.4 collective-permute-start.10
  90.1 5.0 collective-permute-start.26
  95.1 4.8 collective-permute-start.29
  103.8 5.5 collective-permute-start.50
  109.3 4.2 collective-permute-start.53
  117.4 3.6 collective-permute-start.1
  121.7 5.7 collective-permute-start.24
  131.3 3.6 collective-permute-start.8
  151.9 3.4 collective-permute-start.31
  158.7 5.5 collective-permute-start.48
  164.2 4.5 collective-permute-start.25
  168.7 2.1 collective-permute-start.28
  174.1 10.9 %gather_fusion.5 = f32[3072,28]{1,0:T(8,128)} fusion(f32[28,5120]{0,1:T(8,128)S(1)} %copy.321, s32[3072]{0:T(1024)S(1)} %copy-done.60), kind=kCustom, calls=%fused_computation.6 | custom fusion | bytes 700416 | tf_op jit(solution)/shard_map/gather | solution.py:196
  191.6 17.9 %scatter_custom_fusion = f32[28,5120]{0,1:T(8,128)S(1)} fusion(s32[3072]{0:T(1024)} %bitcast.397, f32[3072,28]{1,0:T(8,128)} %copy.327, f32[]{:T(128)} %constant.38.clone.1), kind=kCustom, calls=%fused_computation.36 | custom fusion | flops 86016 | bytes 573952 | tf_op jit(solution)/shard_map/transpose(jvp())/scatter-add | solution.py:76
  213.3 3.4 collective-permute-start.55
  218.7 4.2 collective-permute-start.32
  229.8 3.6 collective-permute-start.49
  235.4 3.6 collective-permute-start.56
  241.0 5.8 collective-permute-start.12
  250.9 11.9 %gather_fusion.9 = f32[3072,28]{1,0:T(8,128)} fusion(f32[28,5120]{0,1:T(8,128)S(1)} %copy.350, s32[3072]{0:T(1024)} %broadcast_clamp_fusion), kind=kCustom, calls=%fused_computation.11 | custom fusion | bytes 700416 | tf_op jit(solution)/shard_map/gather | solution.py:196
  273.7 4.2 collective-permute-start.17
  284.6 11.9 %gather_fusion.13 = f32[3072,28]{1,0:T(8,128)} fusion(f32[28,5120]{0,1:T(8,128)S(1)} %copy.379, s32[3072]{0:T(1024)} %broadcast_clamp_fusion), kind=kCustom, calls=%fused_computation.16 | custom fusion | bytes 700416 | tf_op jit(solution)/shard_map/gather | solution.py:196
  298.8 3.6 collective-permute-start.19
  302.5 3.4 collective-permute-start.22
  308.5 4.2 collective-permute-start.13
  314.7 3.6 collective-permute-start.20
  318.3 2.1 collective-permute-start.23
  334.3 13.9 %scatter_custom_fusion.2 = f32[28,3072]{0,1:T(8,128)S(1)} fusion(s32[2048]{0:T(1024)} %bitcast.407, f32[2048,28]{1,0:T(8,128)} %bitcast.370, f32[]{:T(128)} %constant.38.clone.1), kind=kCustom, calls=%fused_computation.57 | custom fusion | flops 57344 | bytes 344576 | tf_op jit(solution)/shard_map/scatter-add | solution.py:227
  360.8 17.9 %scatter_custom_fusion.4 = f32[28,5120]{0,1:T(8,128)S(1)} fusion(s32[3072]{0:T(1024)} %bitcast.398, f32[3072,28]{1,0:T(8,128)} %copy.356, f32[]{:T(128)} %constant.38.clone.1), kind=kCustom, calls=%fused_computation.34 | custom fusion | flops 86016 | bytes 573952 | tf_op jit(solution)/shard_map/transpose(jvp())/scatter-add | solution.py:76
  381.5 5.7 collective-permute-start.36
  388.8 2.1 collective-permute-start.38
  396.1 4.1 collective-permute-start.41
  403.1 2.3 fusion.116
  410.4 3.6 collective-permute-start.43
  414.1 3.6 collective-permute-start.46
  422.1 4.2 collective-permute-start.37
  428.2 3.6 collective-permute-start.44
  446.3 13.6 %scatter_custom_fusion.6 = f32[28,3072]{0,1:T(8,128)S(1)} fusion(s32[2048]{0:T(1024)} %bitcast.408, f32[2048,28]{1,0:T(8,128)S(1)} %bitcast.371, f32[]{:T(128)} %constant.38.clone.1), kind=kCustom, calls=%fused_computation.55 | custom fusion | flops 57344 | bytes 344576 | tf_op jit(solution)/shard_map/scatter-add | solution.py:227
  472.5 17.9 %scatter_custom_fusion.8 = f32[28,5120]{0,1:T(8,128)S(1)} fusion(s32[3072]{0:T(1024)} %bitcast.399, f32[3072,28]{1,0:T(8,128)} %copy.385, f32[]{:T(128)} %constant.38.clone.1), kind=kCustom, calls=%fused_computation.32 | custom fusion | flops 86016 | bytes 573952 | tf_op jit(solution)/shard_map/transpose(jvp())/scatter-add | solution.py:76
  493.2 5.7 collective-permute-start.60
  500.5 2.3 collective-permute-start.62
  507.0 4.1 collective-permute-start.65
  511.2 2.1 collective-permute-start.66
  518.5 61.0 %all-reduce.42 = (f32[2,512]{0,1:T(8,128)}, f32[2,512]{0,1:T(8,128)}, f32[2,512]{0,1:T(8,128)}) all-reduce(f32[2,512]{0,1:T(8,128)S(1)} %scatter_custom_fusion.14, f32[2,512]{0,1:T(8,128)S(1)} %scatter_custom_fusion.13, f32[2,512]{0,1:T(8,128)} %scatter_custom_fusion.12), channel_id=1, replica_groups=mesh['gx'=16,'gy'=8] {'gx'}, use_global_device_ids=true, to_apply=%region_37.38 | all-reduce | flops 3072 | bytes 24576 | tf_op jit(solution)/shard_map/psum | solution.py:19
  579.5 40.6 %all-reduce.43 = (f32[2,512]{0,1:T(8,128)S(1)}, f32[2,512]{0,1:T(8,128)}, f32[2,512]{0,1:T(8,128)}) all-reduce(f32[2,512]{0,1:T(8,128)} %get-tuple-element.21, f32[2,512]{0,1:T(8,128)} %get-tuple-element.22, f32[2,512]{0,1:T(8,128)} %get-tuple-element.23), channel_id=1, replica_groups=mesh['gx'=16,'gy'=8] {'gy'}, use_global_device_ids=true, to_apply=%region_38.39 | all-reduce | flops 3072 | bytes 24576 | tf_op jit(solution)/shard_map/psum | solution.py:19
  625.3 7.2 %collective-permute-start.67 = (f32[28,256]{1,0:T(8,128)}, f32[28,256]{1,0:T(8,128)}, u32[]{:S(2)}, u32[]{:S(2)}) collective-permute-start(f32[28,256]{1,0:T(8,128)} %bitcast.124), channel_id=1, source_target_pairs={{8,0},{16,8},{24,16},{32,24},{40,32},{48,40},{56,48},{64,56},{72,6... | collective-permute-start | bytes 86024 | tf_op jit(solution)/shard_map/ppermute | solution.py:28
  636.9 6.7 collective-permute-start.69
  643.6 4.0 collective-permute-start.61
  647.6 3.7 collective-permute-start.64
  653.3 2.4 collective-permute-start.71
  665.2 13.6 %scatter_custom_fusion.10 = f32[28,3072]{0,1:T(8,128)S(1)} fusion(s32[2048]{0:T(1024)} %bitcast.409, f32[2048,28]{1,0:T(8,128)S(1)} %bitcast.369, f32[]{:T(128)} %constant.38.clone.1), kind=kCustom, calls=%fused_computation.53 | custom fusion | flops 57344 | bytes 344576 | tf_op jit(solution)/shard_map/scatter-add | solution.py:227
  (693 shorter events, 226.9 us)
Async XLA Ops:
  40.8 41.9 %collective-permute-start = (bf16[1,28,256]{2,1,0:T(8,128)(2,1)}, bf16[1,28,256]{2,1,0:T(8,128)(2,1)}, u32[]{:S(2)}, u32[]{:S(2)}) collective-permute-start(bf16[1,28,256]{2,1,0:T(8,128)(2,1)} %get-tuple-element.118), channel_id=1, source_target_pairs={{0,8},{8,16},{16,24},{24,32},{32,40},{40,48},{48,56},{56,64},{64,7... | collective-permute-start | bytes 43016 | tf_op jit(solution)/shard_map/ppermute | solution.py:28
  44.2 40.6 %collective-permute-start.2 = (bf16[1,28,256]{2,1,0:T(8,128)(2,1)}, bf16[1,28,256]{2,1,0:T(8,128)(2,1)}, u32[]{:S(2)}, u32[]{:S(2)}) collective-permute-start(bf16[1,28,256]{2,1,0:T(8,128)(2,1)} %get-tuple-element.117), channel_id=1, source_target_pairs={{0,8},{8,16},{16,24},{24,32},{32,40},{40,48},{48,56},{56,64},{64,7... | collective-permute-start | bytes 43016 | tf_op jit(solution)/shard_map/ppermute | solution.py:28
  47.4 40.3 %collective-permute-start.3 = (bf16[1,28,256]{2,1,0:T(8,128)(2,1)}, bf16[1,28,256]{2,1,0:T(8,128)(2,1)}, u32[]{:S(2)}, u32[]{:S(2)}) collective-permute-start(bf16[1,28,256]{2,1,0:T(8,128)(2,1)} %get-tuple-element.116), channel_id=1, source_target_pairs={{0,8},{8,16},{16,24},{24,32},{32,40},{40,48},{48,56},{56,64},{64,7... | collective-permute-start | bytes 43016 | tf_op jit(solution)/shard_map/ppermute | solution.py:28
  50.5 39.6 %collective-permute-start.5 = (bf16[1,28,256]{2,1,0:T(8,128)(2,1)}, bf16[1,28,256]{2,1,0:T(8,128)(2,1)}, u32[]{:S(2)}, u32[]{:S(2)}) collective-permute-start(bf16[1,28,256]{2,1,0:T(8,128)(2,1)} %get-tuple-element.115), channel_id=1, source_target_pairs={{0,1},{1,2},{2,3},{3,4},{4,5},{5,6},{6,7},{8,9},{9,10},{10,11},{11... | collective-permute-start | bytes 43016 | tf_op jit(solution)/shard_map/ppermute | solution.py:28
  55.1 40.0 %collective-permute-start.6 = (bf16[1,28,256]{2,1,0:T(8,128)(2,1)}, bf16[1,28,256]{2,1,0:T(8,128)(2,1)}, u32[]{:S(2)}, u32[]{:S(2)}) collective-permute-start(bf16[1,28,256]{2,1,0:T(8,128)(2,1)} %get-tuple-element.114), channel_id=1, source_target_pairs={{1,0},{2,1},{3,2},{4,3},{5,4},{6,5},{7,6},{9,8},{10,9},{11,10},{12... | collective-permute-start | bytes 43016 | tf_op jit(solution)/shard_map/ppermute | solution.py:28
  82.7 17.1 %collective-permute-start.7 = (bf16[1,28,256]{2,1,0:T(8,128)(2,1)S(1)}, bf16[1,28,256]{2,1,0:T(8,128)(2,1)}, u32[]{:S(2)}, u32[]{:S(2)}) collective-permute-start(bf16[1,28,256]{2,1,0:T(8,128)(2,1)S(1)} %copy-done.105), channel_id=1, source_target_pairs={{8,0},{16,8},{24,16},{32,24},{40,32},{48,40},{56,48},{64,56},{72,6... | collective-permute-start | bytes 43016 | tf_op jit(solution)/shard_map/ppermute | solution.py:28
  84.9 16.9 %collective-permute-start.9 = (bf16[1,28,256]{2,1,0:T(8,128)(2,1)S(1)}, bf16[1,28,256]{2,1,0:T(8,128)(2,1)S(1)}, u32[]{:S(2)}, u32[]{:S(2)}) collective-permute-start(bf16[1,28,256]{2,1,0:T(8,128)(2,1)S(1)} %copy-done.104), channel_id=1, source_target_pairs={{8,0},{16,8},{24,16},{32,24},{40,32},{48,40},{56,48},{64,56},{72,6... | collective-permute-start | bytes 43016 | tf_op jit(solution)/shard_map/ppermute | solution.py:28
  87.7 16.1 %collective-permute-start.10 = (bf16[1,28,256]{2,1,0:T(8,128)(2,1)S(1)}, bf16[1,28,256]{2,1,0:T(8,128)(2,1)}, u32[]{:S(2)}, u32[]{:S(2)}) collective-permute-start(bf16[1,28,256]{2,1,0:T(8,128)(2,1)S(1)} %copy-done.103), channel_id=1, source_target_pairs={{8,0},{16,8},{24,16},{32,24},{40,32},{48,40},{56,48},{64,56},{72,6... | collective-permute-start | bytes 43016 | tf_op jit(solution)/shard_map/ppermute | solution.py:28
  90.1 19.2 %collective-permute-start.26 = (bf16[1,28,256]{2,1,0:T(8,128)(2,1)}, bf16[1,28,256]{2,1,0:T(8,128)(2,1)S(1)}, u32[]{:S(2)}, u32[]{:S(2)}) collective-permute-start(bf16[1,28,256]{2,1,0:T(8,128)(2,1)} %get-tuple-element.109), channel_id=1, source_target_pairs={{0,8},{8,16},{16,24},{24,32},{32,40},{40,48},{48,56},{56,64},{64,7... | collective-permute-start | bytes 43016 | tf_op jit(solution)/shard_map/ppermute | solution.py:28
  95.1 18.4 %collective-permute-start.29 = (bf16[1,28,256]{2,1,0:T(8,128)(2,1)}, bf16[1,28,256]{2,1,0:T(8,128)(2,1)S(1)}, u32[]{:S(2)}, u32[]{:S(2)}) collective-permute-start(bf16[1,28,256]{2,1,0:T(8,128)(2,1)} %get-tuple-element.107), channel_id=1, source_target_pairs={{0,1},{1,2},{2,3},{3,4},{4,5},{5,6},{6,7},{8,9},{9,10},{10,11},{11... | collective-permute-start | bytes 43016 | tf_op jit(solution)/shard_map/ppermute | solution.py:28
  103.8 17.9 %collective-permute-start.50 = (bf16[1,28,256]{2,1,0:T(8,128)(2,1)S(1)}, bf16[1,28,256]{2,1,0:T(8,128)(2,1)S(1)}, u32[]{:S(2)}, u32[]{:S(2)}) collective-permute-start(bf16[1,28,256]{2,1,0:T(8,128)(2,1)S(1)} %get-tuple-element.101), channel_id=1, source_target_pairs={{0,8},{8,16},{16,24},{24,32},{32,40},{40,48},{48,56},{56,64},{64,7... | collective-permute-start | bytes 43016 | tf_op jit(solution)/shard_map/ppermute | solution.py:28
  109.3 18.1 %collective-permute-start.53 = (bf16[1,28,256]{2,1,0:T(8,128)(2,1)S(1)}, bf16[1,28,256]{2,1,0:T(8,128)(2,1)S(1)}, u32[]{:S(2)}, u32[]{:S(2)}) collective-permute-start(bf16[1,28,256]{2,1,0:T(8,128)(2,1)S(1)} %get-tuple-element.99), channel_id=1, source_target_pairs={{0,1},{1,2},{2,3},{3,4},{4,5},{5,6},{6,7},{8,9},{9,10},{10,11},{11... | collective-permute-start | bytes 43016 | tf_op jit(solution)/shard_map/ppermute | solution.py:28
  113.5 15.9 %collective-permute-start.54 = (bf16[1,28,256]{2,1,0:T(8,128)(2,1)S(1)}, bf16[1,28,256]{2,1,0:T(8,128)(2,1)S(1)}, u32[]{:S(2)}, u32[]{:S(2)}) collective-permute-start(bf16[1,28,256]{2,1,0:T(8,128)(2,1)S(1)} %get-tuple-element.98), channel_id=1, source_target_pairs={{1,0},{2,1},{3,2},{4,3},{5,4},{6,5},{7,6},{9,8},{10,9},{11,10},{12... | collective-permute-start | bytes 43016 | tf_op jit(solution)/shard_map/ppermute | solution.py:28
  115.5 15.9 %collective-permute-start.57 = (bf16[1,28,256]{2,1,0:T(8,128)(2,1)S(1)}, bf16[1,28,256]{2,1,0:T(8,128)(2,1)S(1)}, u32[]{:S(2)}, u32[]{:S(2)}) collective-permute-start(bf16[1,28,256]{2,1,0:T(8,128)(2,1)S(1)} %get-tuple-element.96), channel_id=1, source_target_pairs={{8,0},{16,8},{24,16},{32,24},{40,32},{48,40},{56,48},{64,56},{72,6... | collective-permute-start | bytes 43016 | tf_op jit(solution)/shard_map/ppermute | solution.py:28
  117.4 17.6 %collective-permute-start.1 = (bf16[1,28,256]{2,1,0:T(8,128)(2,1)}, bf16[1,28,256]{2,1,0:T(8,128)(2,1)S(1)}, u32[]{:S(2)}, u32[]{:S(2)}) collective-permute-start(bf16[1,28,256]{2,1,0:T(8,128)(2,1)} %collective-permute-done), channel_id=1, source_target_pairs={{0,1},{1,2},{2,3},{3,4},{4,5},{5,6},{6,7},{8,9},{9,10},{10,11},{11... | collective-permute-start | bytes 43016 | tf_op jit(solution)/shard_map/ppermute | solution.py:28
  121.7 37.1 %collective-permute-start.24 = (bf16[1,28,256]{2,1,0:T(8,128)(2,1)S(1)}, bf16[1,28,256]{2,1,0:T(8,128)(2,1)}, u32[]{:S(2)}, u32[]{:S(2)}) collective-permute-start(bf16[1,28,256]{2,1,0:T(8,128)(2,1)S(1)} %get-tuple-element.110), channel_id=1, source_target_pairs={{0,8},{8,16},{16,24},{24,32},{32,40},{40,48},{48,56},{56,64},{64,7... | collective-permute-start | bytes 43016 | tf_op jit(solution)/shard_map/ppermute | solution.py:28
  127.4 36.8 %collective-permute-start.27 = (bf16[1,28,256]{2,1,0:T(8,128)(2,1)S(1)}, bf16[1,28,256]{2,1,0:T(8,128)(2,1)}, u32[]{:S(2)}, u32[]{:S(2)}) collective-permute-start(bf16[1,28,256]{2,1,0:T(8,128)(2,1)S(1)} %get-tuple-element.108), channel_id=1, source_target_pairs={{0,8},{8,16},{16,24},{24,32},{32,40},{40,48},{48,56},{56,64},{64,7... | collective-permute-start | bytes 43016 | tf_op jit(solution)/shard_map/ppermute | solution.py:28
  129.4 22.5 %collective-permute-start.4 = (bf16[1,28,256]{2,1,0:T(8,128)(2,1)}, bf16[1,28,256]{2,1,0:T(8,128)(2,1)}, u32[]{:S(2)}, u32[]{:S(2)}) collective-permute-start(bf16[1,28,256]{2,1,0:T(8,128)(2,1)} %collective-permute-done.3), channel_id=1, source_target_pairs={{1,0},{2,1},{3,2},{4,3},{5,4},{6,5},{7,6},{9,8},{10,9},{11,10},{12... | collective-permute-start | bytes 43016 | tf_op jit(solution)/shard_map/ppermute | solution.py:28
  131.3 24.7 %collective-permute-start.8 = (bf16[1,28,256]{2,1,0:T(8,128)(2,1)}, bf16[1,28,256]{2,1,0:T(8,128)(2,1)}, u32[]{:S(2)}, u32[]{:S(2)}) collective-permute-start(bf16[1,28,256]{2,1,0:T(8,128)(2,1)} %collective-permute-done.7), channel_id=1, source_target_pairs={{0,1},{1,2},{2,3},{3,4},{4,5},{5,6},{6,7},{8,9},{9,10},{10,11},{11... | collective-permute-start | bytes 43016 | tf_op jit(solution)/shard_map/ppermute | solution.py:28
  135.0 33.7 %collective-permute-start.11 = (bf16[1,28,256]{2,1,0:T(8,128)(2,1)}, bf16[1,28,256]{2,1,0:T(8,128)(2,1)S(1)}, u32[]{:S(2)}, u32[]{:S(2)}) collective-permute-start(bf16[1,28,256]{2,1,0:T(8,128)(2,1)} %collective-permute-done.10), channel_id=1, source_target_pairs={{1,0},{2,1},{3,2},{4,3},{5,4},{6,5},{7,6},{9,8},{10,9},{11,10},{12... | collective-permute-start | bytes 43016 | tf_op jit(solution)/shard_map/ppermute | solution.py:28
  151.9 59.4 %collective-permute-start.31 = (bf16[1,28,256]{2,1,0:T(8,128)(2,1)}, bf16[1,28,256]{2,1,0:T(8,128)(2,1)}, u32[]{:S(2)}, u32[]{:S(2)}) collective-permute-start(bf16[1,28,256]{2,1,0:T(8,128)(2,1)} %get-tuple-element.105), channel_id=1, source_target_pairs={{8,0},{16,8},{24,16},{32,24},{40,32},{48,40},{56,48},{64,56},{72,6... | collective-permute-start | bytes 43016 | tf_op jit(solution)/shard_map/ppermute | solution.py:28
  156.0 57.3 %collective-permute-start.34 = (bf16[1,28,256]{2,1,0:T(8,128)(2,1)}, bf16[1,28,256]{2,1,0:T(8,128)(2,1)}, u32[]{:S(2)}, u32[]{:S(2)}) collective-permute-start(bf16[1,28,256]{2,1,0:T(8,128)(2,1)} %get-tuple-element.103), channel_id=1, source_target_pairs={{8,0},{16,8},{24,16},{32,24},{40,32},{48,40},{56,48},{64,56},{72,6... | collective-permute-start | bytes 43016 | tf_op jit(solution)/shard_map/ppermute | solution.py:28
  158.7 58.0 %collective-permute-start.48 = (bf16[1,28,256]{2,1,0:T(8,128)(2,1)}, bf16[1,28,256]{2,1,0:T(8,128)(2,1)}, u32[]{:S(2)}, u32[]{:S(2)}) collective-permute-start(bf16[1,28,256]{2,1,0:T(8,128)(2,1)} %get-tuple-element.102), channel_id=1, source_target_pairs={{0,8},{8,16},{16,24},{24,32},{32,40},{40,48},{48,56},{56,64},{64,7... | collective-permute-start | bytes 43016 | tf_op jit(solution)/shard_map/ppermute | solution.py:28
  164.2 54.5 %collective-permute-start.25 = (bf16[1,28,256]{2,1,0:T(8,128)(2,1)}, bf16[1,28,256]{2,1,0:T(8,128)(2,1)}, u32[]{:S(2)}, u32[]{:S(2)}) collective-permute-start(bf16[1,28,256]{2,1,0:T(8,128)(2,1)} %collective-permute-done.24), channel_id=1, source_target_pairs={{0,1},{1,2},{2,3},{3,4},{4,5},{5,6},{6,7},{8,9},{9,10},{10,11},{11... | collective-permute-start | bytes 43016 | tf_op jit(solution)/shard_map/ppermute | solution.py:28
  168.7 54.2 %collective-permute-start.28 = (bf16[1,28,256]{2,1,0:T(8,128)(2,1)}, bf16[1,28,256]{2,1,0:T(8,128)(2,1)}, u32[]{:S(2)}, u32[]{:S(2)}) collective-permute-start(bf16[1,28,256]{2,1,0:T(8,128)(2,1)} %collective-permute-done.27), channel_id=1, source_target_pairs={{1,0},{2,1},{3,2},{4,3},{5,4},{6,5},{7,6},{9,8},{10,9},{11,10},{12... | collective-permute-start | bytes 43016 | tf_op jit(solution)/shard_map/ppermute | solution.py:28
  211.3 18.5 %collective-permute-start.51 = (bf16[1,28,256]{2,1,0:T(8,128)(2,1)}, bf16[1,28,256]{2,1,0:T(8,128)(2,1)}, u32[]{:S(2)}, u32[]{:S(2)}) collective-permute-start(bf16[1,28,256]{2,1,0:T(8,128)(2,1)} %get-tuple-element.100), channel_id=1, source_target_pairs={{0,8},{8,16},{16,24},{24,32},{32,40},{40,48},{48,56},{56,64},{64,7... | collective-permute-start | bytes 43016 | tf_op jit(solution)/shard_map/ppermute | solution.py:28
  213.3 20.1 %collective-permute-start.55 = (bf16[1,28,256]{2,1,0:T(8,128)(2,1)}, bf16[1,28,256]{2,1,0:T(8,128)(2,1)}, u32[]{:S(2)}, u32[]{:S(2)}) collective-permute-start(bf16[1,28,256]{2,1,0:T(8,128)(2,1)} %get-tuple-element.97), channel_id=1, source_target_pairs={{8,0},{16,8},{24,16},{32,24},{40,32},{48,40},{56,48},{64,56},{72,6... | collective-permute-start | bytes 43016 | tf_op jit(solution)/shard_map/ppermute | solution.py:28
  216.7 18.7 %collective-permute-start.58 = (bf16[1,28,256]{2,1,0:T(8,128)(2,1)}, bf16[1,28,256]{2,1,0:T(8,128)(2,1)}, u32[]{:S(2)}, u32[]{:S(2)}) collective-permute-start(bf16[1,28,256]{2,1,0:T(8,128)(2,1)} %get-tuple-element.95), channel_id=1, source_target_pairs={{8,0},{16,8},{24,16},{32,24},{40,32},{48,40},{56,48},{64,56},{72,6... | collective-permute-start | bytes 43016 | tf_op jit(solution)/shard_map/ppermute | solution.py:28
  218.7 20.4 %collective-permute-start.32 = (bf16[1,28,256]{2,1,0:T(8,128)(2,1)}, bf16[1,28,256]{2,1,0:T(8,128)(2,1)S(1)}, u32[]{:S(2)}, u32[]{:S(2)}) collective-permute-start(bf16[1,28,256]{2,1,0:T(8,128)(2,1)} %collective-permute-done.31), channel_id=1, source_target_pairs={{0,1},{1,2},{2,3},{3,4},{4,5},{5,6},{6,7},{8,9},{9,10},{10,11},{11... | collective-permute-start | bytes 43016 | tf_op jit(solution)/shard_map/ppermute | solution.py:28
  222.9 18.2 %collective-permute-start.35 = (bf16[1,28,256]{2,1,0:T(8,128)(2,1)}, bf16[1,28,256]{2,1,0:T(8,128)(2,1)S(1)}, u32[]{:S(2)}, u32[]{:S(2)}) collective-permute-start(bf16[1,28,256]{2,1,0:T(8,128)(2,1)} %collective-permute-done.34), channel_id=1, source_target_pairs={{1,0},{2,1},{3,2},{4,3},{5,4},{6,5},{7,6},{9,8},{10,9},{11,10},{12... | collective-permute-start | bytes 43016 | tf_op jit(solution)/shard_map/ppermute | solution.py:28
  229.8 38.5 %collective-permute-start.49 = (bf16[1,28,256]{2,1,0:T(8,128)(2,1)}, bf16[1,28,256]{2,1,0:T(8,128)(2,1)}, u32[]{:S(2)}, u32[]{:S(2)}) collective-permute-start(bf16[1,28,256]{2,1,0:T(8,128)(2,1)} %collective-permute-done.48), channel_id=1, source_target_pairs={{0,1},{1,2},{2,3},{3,4},{4,5},{5,6},{6,7},{8,9},{9,10},{10,11},{11... | collective-permute-start | bytes 43016 | tf_op jit(solution)/shard_map/ppermute | solution.py:28
  233.5 37.5 %collective-permute-start.52 = (bf16[1,28,256]{2,1,0:T(8,128)(2,1)}, bf16[1,28,256]{2,1,0:T(8,128)(2,1)}, u32[]{:S(2)}, u32[]{:S(2)}) collective-permute-start(bf16[1,28,256]{2,1,0:T(8,128)(2,1)} %collective-permute-done.51), channel_id=1, source_target_pairs={{1,0},{2,1},{3,2},{4,3},{5,4},{6,5},{7,6},{9,8},{10,9},{11,10},{12... | collective-permute-start | bytes 43016 | tf_op jit(solution)/shard_map/ppermute | solution.py:28
  235.4 38.3 %collective-permute-start.56 = (bf16[1,28,256]{2,1,0:T(8,128)(2,1)}, bf16[1,28,256]{2,1,0:T(8,128)(2,1)}, u32[]{:S(2)}, u32[]{:S(2)}) collective-permute-start(bf16[1,28,256]{2,1,0:T(8,128)(2,1)} %collective-permute-done.55), channel_id=1, source_target_pairs={{0,1},{1,2},{2,3},{3,4},{4,5},{5,6},{6,7},{8,9},{9,10},{10,11},{11... | collective-permute-start | bytes 43016 | tf_op jit(solution)/shard_map/ppermute | solution.py:28
  239.1 39.6 %collective-permute-start.59 = (bf16[1,28,256]{2,1,0:T(8,128)(2,1)}, bf16[1,28,256]{2,1,0:T(8,128)(2,1)}, u32[]{:S(2)}, u32[]{:S(2)}) collective-permute-start(bf16[1,28,256]{2,1,0:T(8,128)(2,1)} %collective-permute-done.58), channel_id=1, source_target_pairs={{1,0},{2,1},{3,2},{4,3},{5,4},{6,5},{7,6},{9,8},{10,9},{11,10},{12... | collective-permute-start | bytes 43016 | tf_op jit(solution)/shard_map/ppermute | solution.py:28
  241.0 57.8 %collective-permute-start.12 = (f32[28,256]{1,0:T(8,128)}, f32[28,256]{1,0:T(8,128)}, u32[]{:S(2)}, u32[]{:S(2)}) collective-permute-start(f32[28,256]{1,0:T(8,128)} %bitcast.43), channel_id=1, source_target_pairs={{0,8},{8,16},{16,24},{24,32},{32,40},{40,48},{48,56},{56,64},{64,7... | collective-permute-start | bytes 86024 | tf_op jit(solution)/shard_map/ppermute | solution.py:28
  268.3 34.1 %collective-permute-start.14 = (f32[28,256]{1,0:T(8,128)}, f32[28,256]{1,0:T(8,128)}, u32[]{:S(2)}, u32[]{:S(2)}) collective-permute-start(f32[28,256]{1,0:T(8,128)} %bitcast.44), channel_id=1, source_target_pairs={{0,8},{8,16},{16,24},{24,32},{32,40},{40,48},{48,56},{56,64},{64,7... | collective-permute-start | bytes 86024 | tf_op jit(solution)/shard_map/ppermute | solution.py:28
  271.0 35.6 %collective-permute-start.15 = (f32[28,256]{1,0:T(8,128)}, f32[28,256]{1,0:T(8,128)}, u32[]{:S(2)}, u32[]{:S(2)}) collective-permute-start(f32[28,256]{1,0:T(8,128)} %bitcast.45), channel_id=1, source_target_pairs={{0,8},{8,16},{16,24},{24,32},{32,40},{40,48},{48,56},{56,64},{64,7... | collective-permute-start | bytes 86024 | tf_op jit(solution)/shard_map/ppermute | solution.py:28
  273.7 34.8 %collective-permute-start.17 = (f32[28,256]{1,0:T(8,128)}, f32[28,256]{1,0:T(8,128)}, u32[]{:S(2)}, u32[]{:S(2)}) collective-permute-start(f32[28,256]{1,0:T(8,128)} %bitcast.46), channel_id=1, source_target_pairs={{0,1},{1,2},{2,3},{3,4},{4,5},{5,6},{6,7},{8,9},{9,10},{10,11},{11... | collective-permute-start | bytes 86024 | tf_op jit(solution)/shard_map/ppermute | solution.py:28
  278.7 34.1 %collective-permute-start.18 = (f32[28,256]{1,0:T(8,128)}, f32[28,256]{1,0:T(8,128)}, u32[]{:S(2)}, u32[]{:S(2)}) collective-permute-start(f32[28,256]{1,0:T(8,128)} %bitcast.47), channel_id=1, source_target_pairs={{1,0},{2,1},{3,2},{4,3},{5,4},{6,5},{7,6},{9,8},{10,9},{11,10},{12... | collective-permute-start | bytes 86024 | tf_op jit(solution)/shard_map/ppermute | solution.py:28
  298.8 15.8 %collective-permute-start.19 = (f32[28,256]{1,0:T(8,128)S(1)}, f32[28,256]{1,0:T(8,128)}, u32[]{:S(2)}, u32[]{:S(2)}) collective-permute-start(f32[28,256]{1,0:T(8,128)S(1)} %bitcast.405), channel_id=1, source_target_pairs={{8,0},{16,8},{24,16},{32,24},{40,32},{48,40},{56,48},{64,56},{72,6... | collective-permute-start | bytes 86024 | tf_op jit(solution)/shard_map/ppermute | solution.py:28
  306.6 25.0 %collective-permute-start.21 = (f32[28,256]{1,0:T(8,128)}, f32[28,256]{1,0:T(8,128)S(1)}, u32[]{:S(2)}, u32[]{:S(2)}) collective-permute-start(f32[28,256]{1,0:T(8,128)} %bitcast.49), channel_id=1, source_target_pairs={{8,0},{16,8},{24,16},{32,24},{40,32},{48,40},{56,48},{64,56},{72,6... | collective-permute-start | bytes 86024 | tf_op jit(solution)/shard_map/ppermute | solution.py:28
  308.5 23.1 %collective-permute-start.13 = (f32[28,256]{1,0:T(8,128)}, f32[28,256]{1,0:T(8,128)S(1)}, u32[]{:S(2)}, u32[]{:S(2)}) collective-permute-start(f32[28,256]{1,0:T(8,128)} %collective-permute-done.12), channel_id=1, source_target_pairs={{0,1},{1,2},{2,3},{3,4},{4,5},{5,6},{6,7},{8,9},{9,10},{10,11},{11... | collective-permute-start | bytes 86024 | tf_op jit(solution)/shard_map/ppermute | solution.py:28
  312.7 18.9 %collective-permute-start.16 = (f32[28,256]{1,0:T(8,128)}, f32[28,256]{1,0:T(8,128)S(1)}, u32[]{:S(2)}, u32[]{:S(2)}) collective-permute-start(f32[28,256]{1,0:T(8,128)} %collective-permute-done.15), channel_id=1, source_target_pairs={{1,0},{2,1},{3,2},{4,3},{5,4},{6,5},{7,6},{9,8},{10,9},{11,10},{12... | collective-permute-start | bytes 86024 | tf_op jit(solution)/shard_map/ppermute | solution.py:28
  314.7 17.0 %collective-permute-start.20 = (f32[28,256]{1,0:T(8,128)}, f32[28,256]{1,0:T(8,128)S(1)}, u32[]{:S(2)}, u32[]{:S(2)}) collective-permute-start(f32[28,256]{1,0:T(8,128)} %collective-permute-done.19), channel_id=1, source_target_pairs={{0,1},{1,2},{2,3},{3,4},{4,5},{5,6},{6,7},{8,9},{9,10},{10,11},{11... | collective-permute-start | bytes 86024 | tf_op jit(solution)/shard_map/ppermute | solution.py:28
  381.5 28.9 %collective-permute-start.36 = (f32[28,256]{1,0:T(8,128)}, f32[28,256]{1,0:T(8,128)}, u32[]{:S(2)}, u32[]{:S(2)}) collective-permute-start(f32[28,256]{1,0:T(8,128)} %bitcast.81), channel_id=1, source_target_pairs={{0,8},{8,16},{16,24},{24,32},{32,40},{40,48},{48,56},{56,64},{64,7... | collective-permute-start | bytes 86024 | tf_op jit(solution)/shard_map/ppermute | solution.py:28
  388.8 25.2 %collective-permute-start.38 = (f32[28,256]{1,0:T(8,128)}, f32[28,256]{1,0:T(8,128)}, u32[]{:S(2)}, u32[]{:S(2)}) collective-permute-start(f32[28,256]{1,0:T(8,128)} %bitcast.82), channel_id=1, source_target_pairs={{0,8},{8,16},{16,24},{24,32},{32,40},{40,48},{48,56},{56,64},{64,7... | collective-permute-start | bytes 86024 | tf_op jit(solution)/shard_map/ppermute | solution.py:28
  392.6 27.6 %collective-permute-start.39 = (f32[28,256]{1,0:T(8,128)}, f32[28,256]{1,0:T(8,128)}, u32[]{:S(2)}, u32[]{:S(2)}) collective-permute-start(f32[28,256]{1,0:T(8,128)} %bitcast.83), channel_id=1, source_target_pairs={{0,8},{8,16},{16,24},{24,32},{32,40},{40,48},{48,56},{56,64},{64,7... | collective-permute-start | bytes 86024 | tf_op jit(solution)/shard_map/ppermute | solution.py:28
  396.1 26.0 %collective-permute-start.41 = (f32[28,256]{1,0:T(8,128)}, f32[28,256]{1,0:T(8,128)}, u32[]{:S(2)}, u32[]{:S(2)}) collective-permute-start(f32[28,256]{1,0:T(8,128)} %bitcast.84), channel_id=1, source_target_pairs={{0,1},{1,2},{2,3},{3,4},{4,5},{5,6},{6,7},{8,9},{9,10},{10,11},{11... | collective-permute-start | bytes 86024 | tf_op jit(solution)/shard_map/ppermute | solution.py:28
  401.1 25.1 %collective-permute-start.42 = (f32[28,256]{1,0:T(8,128)S(1)}, f32[28,256]{1,0:T(8,128)}, u32[]{:S(2)}, u32[]{:S(2)}) collective-permute-start(f32[28,256]{1,0:T(8,128)S(1)} %bitcast.403), channel_id=1, source_target_pairs={{1,0},{2,1},{3,2},{4,3},{5,4},{6,5},{7,6},{9,8},{10,9},{11,10},{12... | collective-permute-start | bytes 86024 | tf_op jit(solution)/shard_map/ppermute | solution.py:28
  410.4 17.8 %collective-permute-start.43 = (f32[28,256]{1,0:T(8,128)}, f32[28,256]{1,0:T(8,128)}, u32[]{:S(2)}, u32[]{:S(2)}) collective-permute-start(f32[28,256]{1,0:T(8,128)} %bitcast.86), channel_id=1, source_target_pairs={{8,0},{16,8},{24,16},{32,24},{40,32},{48,40},{56,48},{64,56},{72,6... | collective-permute-start | bytes 86024 | tf_op jit(solution)/shard_map/ppermute | solution.py:28
  414.1 17.8 %collective-permute-start.46 = (f32[28,256]{1,0:T(8,128)}, f32[28,256]{1,0:T(8,128)}, u32[]{:S(2)}, u32[]{:S(2)}) collective-permute-start(f32[28,256]{1,0:T(8,128)} %bitcast.88), channel_id=1, source_target_pairs={{8,0},{16,8},{24,16},{32,24},{40,32},{48,40},{56,48},{64,56},{72,6... | collective-permute-start | bytes 86024 | tf_op jit(solution)/shard_map/ppermute | solution.py:28
  420.1 21.5 %collective-permute-start.45 = (f32[28,256]{1,0:T(8,128)}, f32[28,256]{1,0:T(8,128)}, u32[]{:S(2)}, u32[]{:S(2)}) collective-permute-start(f32[28,256]{1,0:T(8,128)} %bitcast.87), channel_id=1, source_target_pairs={{8,0},{16,8},{24,16},{32,24},{40,32},{48,40},{56,48},{64,56},{72,6... | collective-permute-start | bytes 86024 | tf_op jit(solution)/shard_map/ppermute | solution.py:28
  422.1 20.4 %collective-permute-start.37 = (f32[28,256]{1,0:T(8,128)}, f32[28,256]{1,0:T(8,128)}, u32[]{:S(2)}, u32[]{:S(2)}) collective-permute-start(f32[28,256]{1,0:T(8,128)} %collective-permute-done.36), channel_id=1, source_target_pairs={{0,1},{1,2},{2,3},{3,4},{4,5},{5,6},{6,7},{8,9},{9,10},{10,11},{11... | collective-permute-start | bytes 86024 | tf_op jit(solution)/shard_map/ppermute | solution.py:28
  426.3 16.9 %collective-permute-start.40 = (f32[28,256]{1,0:T(8,128)}, f32[28,256]{1,0:T(8,128)}, u32[]{:S(2)}, u32[]{:S(2)}) collective-permute-start(f32[28,256]{1,0:T(8,128)} %collective-permute-done.39), channel_id=1, source_target_pairs={{1,0},{2,1},{3,2},{4,3},{5,4},{6,5},{7,6},{9,8},{10,9},{11,10},{12... | collective-permute-start | bytes 86024 | tf_op jit(solution)/shard_map/ppermute | solution.py:28
  493.2 132.1 %collective-permute-start.60 = (f32[28,256]{1,0:T(8,128)}, f32[28,256]{1,0:T(8,128)}, u32[]{:S(2)}, u32[]{:S(2)}) collective-permute-start(f32[28,256]{1,0:T(8,128)} %bitcast.119), channel_id=1, source_target_pairs={{0,8},{8,16},{16,24},{24,32},{32,40},{40,48},{48,56},{56,64},{64,7... | collective-permute-start | bytes 86024 | tf_op jit(solution)/shard_map/ppermute | solution.py:28
  500.5 132.0 %collective-permute-start.62 = (f32[28,256]{1,0:T(8,128)}, f32[28,256]{1,0:T(8,128)}, u32[]{:S(2)}, u32[]{:S(2)}) collective-permute-start(f32[28,256]{1,0:T(8,128)} %bitcast.120), channel_id=1, source_target_pairs={{0,8},{8,16},{16,24},{24,32},{32,40},{40,48},{48,56},{56,64},{64,7... | collective-permute-start | bytes 86024 | tf_op jit(solution)/shard_map/ppermute | solution.py:28
  504.4 132.5 %collective-permute-start.63 = (f32[28,256]{1,0:T(8,128)}, f32[28,256]{1,0:T(8,128)}, u32[]{:S(2)}, u32[]{:S(2)}) collective-permute-start(f32[28,256]{1,0:T(8,128)} %bitcast.121), channel_id=1, source_target_pairs={{0,8},{8,16},{16,24},{24,32},{32,40},{40,48},{48,56},{56,64},{64,7... | collective-permute-start | bytes 86024 | tf_op jit(solution)/shard_map/ppermute | solution.py:28
  507.0 136.6 %collective-permute-start.65 = (f32[28,256]{1,0:T(8,128)}, f32[28,256]{1,0:T(8,128)}, u32[]{:S(2)}, u32[]{:S(2)}) collective-permute-start(f32[28,256]{1,0:T(8,128)} %bitcast.122), channel_id=1, source_target_pairs={{0,1},{1,2},{2,3},{3,4},{4,5},{5,6},{6,7},{8,9},{9,10},{10,11},{11... | collective-permute-start | bytes 86024 | tf_op jit(solution)/shard_map/ppermute | solution.py:28
  511.2 136.4 %collective-permute-start.66 = (f32[28,256]{1,0:T(8,128)S(1)}, f32[28,256]{1,0:T(8,128)}, u32[]{:S(2)}, u32[]{:S(2)}) collective-permute-start(f32[28,256]{1,0:T(8,128)S(1)} %bitcast.402), channel_id=1, source_target_pairs={{1,0},{2,1},{3,2},{4,3},{5,4},{6,5},{7,6},{9,8},{10,9},{11,10},{12... | collective-permute-start | bytes 86024 | tf_op jit(solution)/shard_map/ppermute | solution.py:28
  625.3 26.0 %collective-permute-start.67 = (f32[28,256]{1,0:T(8,128)}, f32[28,256]{1,0:T(8,128)}, u32[]{:S(2)}, u32[]{:S(2)}) collective-permute-start(f32[28,256]{1,0:T(8,128)} %bitcast.124), channel_id=1, source_target_pairs={{8,0},{16,8},{24,16},{32,24},{40,32},{48,40},{56,48},{64,56},{72,6... | collective-permute-start | bytes 86024 | tf_op jit(solution)/shard_map/ppermute | solution.py:28
  632.5 20.7 %collective-permute-start.70 = (f32[28,256]{1,0:T(8,128)}, f32[28,256]{1,0:T(8,128)}, u32[]{:S(2)}, u32[]{:S(2)}) collective-permute-start(f32[28,256]{1,0:T(8,128)} %bitcast.126), channel_id=1, source_target_pairs={{8,0},{16,8},{24,16},{32,24},{40,32},{48,40},{56,48},{64,56},{72,6... | collective-permute-start | bytes 86024 | tf_op jit(solution)/shard_map/ppermute | solution.py:28
  636.9 26.6 %collective-permute-start.69 = (f32[28,256]{1,0:T(8,128)}, f32[28,256]{1,0:T(8,128)S(1)}, u32[]{:S(2)}, u32[]{:S(2)}) collective-permute-start(f32[28,256]{1,0:T(8,128)} %bitcast.125), channel_id=1, source_target_pairs={{8,0},{16,8},{24,16},{32,24},{40,32},{48,40},{56,48},{64,56},{72,6... | collective-permute-start | bytes 86024 | tf_op jit(solution)/shard_map/ppermute | solution.py:28
  643.6 20.0 %collective-permute-start.61 = (f32[28,256]{1,0:T(8,128)}, f32[28,256]{1,0:T(8,128)S(1)}, u32[]{:S(2)}, u32[]{:S(2)}) collective-permute-start(f32[28,256]{1,0:T(8,128)} %collective-permute-done.60), channel_id=1, source_target_pairs={{0,1},{1,2},{2,3},{3,4},{4,5},{5,6},{6,7},{8,9},{9,10},{10,11},{11... | collective-permute-start | bytes 86024 | tf_op jit(solution)/shard_map/ppermute | solution.py:28
  647.6 16.0 %collective-permute-start.64 = (f32[28,256]{1,0:T(8,128)}, f32[28,256]{1,0:T(8,128)S(1)}, u32[]{:S(2)}, u32[]{:S(2)}) collective-permute-start(f32[28,256]{1,0:T(8,128)} %collective-permute-done.63), channel_id=1, source_target_pairs={{1,0},{2,1},{3,2},{4,3},{5,4},{6,5},{7,6},{9,8},{10,9},{11,10},{12... | collective-permute-start | bytes 86024 | tf_op jit(solution)/shard_map/ppermute | solution.py:28
  (161 other events, 2237.8 us)
